TPU v7x, 32 devices: a whole 2x2x4 slice. The times are simulated.
32 devices in a mesh: tm: 32 (over z, y, x, core).
Axes of the slice: x: 2, y: 2, z: 4, core: 2. Of those that a mesh axis runs over, the one named last changes fastest.
Arguments:
- hidden: bfloat16 [12288, 8192], P('tm'), may hold values from -6 to 6
- norm_gain: float32 [8192], replicated, may hold values from 0.1 to 1.9
- w_in: bfloat16 [8192, 768], replicated, may hold values from -0.0625 to 0.0625
- w_short: float32 [768, 7], replicated, may hold values from -2 to 2
- residues: float32 [8, 16], replicated, may hold values from -4 to 4
- rates: float32 [8, 16], replicated, may hold values from 1.6276042e-05 to 0.0333333333, as said below
- skip: float32 [256], replicated, may hold values from -4 to 4
- w_out: bfloat16 [256, 8192], replicated, may hold values from -0.375 to 0.375
Outputs:
- mixed: bfloat16 [12288, 8192], P('tm')
Inputs may be any that keep to these rules, and one draw needn't show every extreme that they name: `rates`: every rate is positive.
All inputs are finite; a program needn't handle non-finite values.
Results may differ from a plain program's by a relative error of at most 0.0088.
Values may be sent and summed in bfloat16 or wider, within the bound.
A program may use at most 256 MiB of HBM per device.

v0:
```python
import functools

import jax
import jax.numpy as jnp
from jax import lax
from jax.experimental import pallas as pl
from jax.experimental.pallas import tpu as pltpu
from jax.sharding import PartitionSpec as P

HIGHEST = lax.Precision.HIGHEST
MESH = pl.DeviceIdType.MESH
LANES = 128
EDGE = 8
F32 = jnp.float32
BF16 = jnp.bfloat16


def iota(shape, dim):
    return lax.broadcasted_iota(jnp.int32, shape, dim)


def dot(a, b):
    return jnp.dot(a, b, preferred_element_type=F32)


def split(x):
    high = x.astype(BF16)
    return high, (x - high.astype(F32)).astype(BF16)


def mixer(
    n, depth, hidden, w_in, gain, taps, rates, residues, skip, out,
    held, w_kv, w_q, acc_kv, acc_q, squares, proj_kv, proj_q, prod, feat_q,
    fall, rise, lag_row, toeplitz, own, slots,
    held_sem, kv_sem, q_sem, edge_sem, send_sem, recv_sem,
):
    me = lax.axis_index("tm")
    following = lax.rem(me + 1, n)
    tok, width = hidden.shape
    chan = prod.shape[1]
    groups, modes = rates.shape
    every = groups * modes
    per_group = chan // groups
    chunks = width // depth

    barrier = pltpu.get_barrier_semaphore()

    @pl.loop(0, me)
    def _(d):
        pl.semaphore_signal(barrier, inc=1, device_id=(d,), device_id_type=MESH)

    def held_copy(k):
        cols = pl.ds(pl.multiple_of(k * depth, depth), depth)
        return pltpu.make_async_copy(hidden.at[:, cols], held.at[k], held_sem.at[k])

    def kv_copy(k):
        rows = pl.ds(pl.multiple_of(k * depth, depth), depth)
        return pltpu.make_async_copy(w_in.at[rows, pl.ds(chan, 2 * chan)], w_kv.at[k], kv_sem.at[k])

    def q_copy(k):
        rows = pl.ds(pl.multiple_of(k * depth, depth), depth)
        return pltpu.make_async_copy(w_in.at[rows, pl.ds(0, chan)], w_q.at[k], q_sem.at[k])

    @pl.loop(0, chunks)
    def _(k):
        held_copy(k).start()
        kv_copy(k).start()

    @pl.loop(0, chunks)
    def _(k):
        q_copy(k).start()

    pick = (iota((modes, every), 1) % modes == iota((modes, every), 0)).astype(F32)
    mine = iota((groups, every), 1) // modes == iota((groups, every), 0)
    spread = (iota((groups, chan), 1) // per_group == iota((groups, chan), 0)).astype(F32)
    diagonal = iota((every, every), 0) == iota((every, every), 1)
    weights = residues[...] * jnp.sqrt(2.0 * rates[...])

    def as_row(x):
        wide = jnp.dot(x, pick, precision=HIGHEST, preferred_element_type=F32)
        return jnp.sum(jnp.where(mine, wide, 0.0), axis=0, keepdims=True)

    def as_column(row):
        return jnp.sum(jnp.where(diagonal, row, 0.0), axis=1, keepdims=True)

    def by_channel(x):
        return lax.dot_general(
            x, spread, (((0,), (0,)), ((), ())), precision=HIGHEST, preferred_element_type=F32
        )

    rate_row = as_row(rates[...])
    rate_col = as_column(rate_row)
    weight_col = as_column(as_row(weights))
    rate_mc = by_channel(rates[...])
    weight_mc = by_channel(weights)
    high, low = split(jnp.exp(-rate_col * (tok - 1 - iota((every, tok), 1)).astype(F32)))
    fall[:every], fall[every:] = high, low
    high, low = split(jnp.exp(-rate_row * (iota((tok, every), 0) + 1).astype(F32)))
    rise[:, :every], rise[:, every:] = high, low
    back = lax.rem(tok - iota((every, tok), 1), tok).astype(F32)
    terms = weight_col * jnp.exp(-rate_col * back)
    for g in range(groups):
        lag_row[g : g + 1] = jnp.sum(terms[g * modes : (g + 1) * modes], axis=0, keepdims=True)

    acc_kv[...] = jnp.zeros_like(acc_kv)
    acc_q[...] = jnp.zeros_like(acc_q)
    squares[...] = jnp.zeros_like(squares)

    @pl.loop(0, chunks)
    def _(k):
        held_copy(k).wait()
        kv_copy(k).wait()
        scale = gain[:, pl.ds(pl.multiple_of(k * depth, depth), depth)]
        parts = []
        for r in range(0, tok, 16):
            x = held[k, r : r + 16].astype(F32)
            sq = x * x
            total = squares[r : r + 16]
            for j in range(0, depth, LANES):
                total = total + sq[:, j : j + LANES]
            squares[r : r + 16] = total
            parts.append((x * scale).astype(BF16))
        scaled = jnp.concatenate(parts, axis=0)
        held[k] = scaled
        acc_kv[...] += dot(scaled, w_kv[k])

    inv = lax.rsqrt(jnp.sum(squares[...], axis=1, keepdims=True) / width + 1e-06)
    proj_kv[EDGE:] = acc_kv[...] * inv

    @pl.when(me == 0)
    def _():
        proj_kv[:EDGE] = jnp.zeros((EDGE, 2 * chan), F32)
        proj_q[:EDGE] = jnp.zeros((EDGE, chan), F32)

    @pl.when(me < n - 1)
    def _():
        pl.semaphore_wait(barrier, n - 1 - me)

    def edge_copy(buf, i):
        return pltpu.make_async_remote_copy(
            src_ref=buf.at[pl.ds(tok, EDGE)], dst_ref=buf.at[pl.ds(0, EDGE)],
            send_sem=edge_sem.at[2 * i], recv_sem=edge_sem.at[2 * i + 1],
            device_id=(following,), device_id_type=MESH,
        )

    @pl.when(me < n - 1)
    def _():
        edge_copy(proj_kv, 0).start()

    half = chunks // 2
    strip = tok // half

    def feature(buf, r, rows, first, tap_first):
        total = jnp.zeros((rows, chan), F32)
        for t in range(taps.shape[0]):
            total = total + taps[t : t + 1, tap_first : tap_first + chan] * buf[
                pl.ds(r + EDGE - t, rows), first : first + chan
            ]
        return total

    def query_step(k, start):
        q_copy(k).wait()
        for r in range(0, strip, 32):
            keyed = feature(proj_kv, start + r, 32, 0, chan)
            valued = feature(proj_kv, start + r, 32, chan, 2 * chan)
            prod[pl.ds(start + r, 32)] = (keyed * valued).astype(BF16)
        acc_q[...] += dot(held[k], w_q[k])

    tiles = tok // LANES
    causal = iota((LANES, LANES), 0) >= iota((LANES, LANES), 1)
    share = groups // (chunks - half)

    def toeplitz_step(k):
        q_copy(k).wait()
        for e in range(share):
            g = (k - half) * share + e
            first = jnp.broadcast_to(lag_row[pl.ds(g, 1)], (LANES, tok))
            moved = pltpu.roll(first, 0, 1, stride=1, stride_axis=0)
            lags = []
            for i in range(tiles):
                at = (tiles - i) % tiles * LANES
                tile = moved[:, at : at + LANES]
                lags.append((jnp.where(causal, tile, 0.0) if i == 0 else tile).astype(BF16))
            for i in range(tiles):
                for j in range(tiles):
                    value = lags[i - j] if i >= j else jnp.zeros((LANES, LANES), BF16)
                    toeplitz[g, i * LANES : (i + 1) * LANES, j * LANES : (j + 1) * LANES] = value
        acc_q[...] += dot(held[k], w_q[k])

    for k in range(1, half):
        query_step(k, k * strip)

    early = half + (chunks - half) // 2

    pl.loop(half, early)(toeplitz_step)

    @pl.when(me > 0)
    def _():
        edge_copy(proj_kv, 0).wait_recv()

    query_step(0, 0)

    both = dot(fall[...], prod[...])
    wide = both[:every] + both[every:]
    group_of = iota((modes, chan), 1) // per_group
    packed = jnp.zeros((modes, chan), F32)
    for g in range(groups):
        packed = packed + jnp.where(group_of == g, wide[g * modes : (g + 1) * modes], 0.0)
    own[...] = packed.astype(BF16)

    def state_copy(source, target):
        return pltpu.make_async_remote_copy(
            src_ref=own, dst_ref=slots.at[source],
            send_sem=send_sem.at[target], recv_sem=recv_sem.at[source],
            device_id=(target,), device_id_type=MESH,
        )

    @pl.loop(me + 1, n)
    def _(d):
        state_copy(me, d).start()

    pl.loop(early, chunks)(toeplitz_step)

    proj_q[EDGE:] = acc_q[...] * inv

    @pl.when(me < n - 1)
    def _():
        edge_copy(proj_q, 1).start()

    product = prod[...]
    channel_group = iota((tok, chan), 1) // per_group
    block = 2 * LANES

    def convolve(some):
        total = []
        for s0 in range(0, tok, block):
            s1 = min(s0 + block, tok)
            here = None
            for g in some:
                part = jnp.where(channel_group[s0:s1] == g, product[s0:s1], jnp.zeros_like(product[s0:s1]))
                term = dot(toeplitz[g, s0:, s0:s1], part)
                here = term if here is None else here + term
            total.append((s0, here))
        return total

    def add(parts):
        for s0, value in parts:
            acc_q[s0:] += value

    acc_q[...] = skip[...] * product.astype(F32)
    add(convolve(range(groups // 2)))

    for r in range(32, tok, 32):
        feat_q[r : r + 32] = feature(proj_q, r, 32, 0, 0)
    add(convolve(range(groups // 2, groups)))

    decay = jnp.exp(-rate_mc * float(tok))

    def gather(d, state):
        state_copy(d, following).wait_recv()
        return decay * state + slots[d].astype(F32)

    @pl.when(me > 0)
    def _():
        edge_copy(proj_q, 1).wait_recv()

    feat_q[:32] = feature(proj_q, 0, 32, 0, 0)
    state = lax.fori_loop(0, me, gather, jnp.zeros((modes, chan), F32)) * weight_mc
    stacked = jnp.concatenate([state] * groups, axis=0)
    same = iota((every, chan), 0) // modes == iota((every, chan), 1) // per_group
    high, low = split(jnp.where(same, stacked, 0.0))
    far = dot(rise[...], jnp.concatenate([high, high], axis=0)) + dot(rise[:, :every], low)
    out[...] = (feat_q[...] * (acc_q[...] + far)).astype(BF16)

    @pl.when(me < n - 1)
    def _():
        edge_copy(proj_kv, 0).wait_send()
        edge_copy(proj_q, 1).wait_send()

    @pl.loop(me + 1, n)
    def _(d):
        state_copy(me, d).wait_send()


def project_out(gated, w_out, mixed):
    block = mixed.shape[1]
    cols = pl.ds(pl.multiple_of(pl.program_id(0) * block, block), block)
    mixed[...] = dot(gated[...], w_out[:, cols]).astype(BF16)


def on_device(n, hidden, norm_gain, w_in, w_short, residues, rates, skip, w_out):
    tok, width = hidden.shape
    chan = w_short.shape[0] // 3
    groups, modes = rates.shape
    every = groups * modes
    depth = min(1024, width)
    chunks = width // depth
    vmem = pl.BlockSpec(memory_space=pltpu.VMEM)
    in_hbm = pl.BlockSpec(memory_space=pltpu.HBM)
    gated = pl.pallas_call(
        functools.partial(mixer, n, depth),
        out_shape=jax.ShapeDtypeStruct((tok, chan), BF16),
        in_specs=[in_hbm, in_hbm] + [vmem] * 5,
        out_specs=vmem,
        scratch_shapes=[
            pltpu.VMEM((chunks, tok, depth), BF16),
            pltpu.VMEM((chunks, depth, 2 * chan), BF16),
            pltpu.VMEM((chunks, depth, chan), BF16),
            pltpu.VMEM((tok, 2 * chan), F32),
            pltpu.VMEM((tok, chan), F32),
            pltpu.VMEM((tok, LANES), F32),
            pltpu.VMEM((EDGE + tok, 2 * chan), F32),
            pltpu.VMEM((EDGE + tok, chan), F32),
            pltpu.VMEM((tok, chan), BF16),
            pltpu.VMEM((tok, chan), F32),
            pltpu.VMEM((2 * every, tok), BF16),
            pltpu.VMEM((tok, 2 * every), BF16),
            pltpu.VMEM((groups, tok), F32),
            pltpu.VMEM((groups, tok, tok), BF16),
            pltpu.VMEM((modes, chan), BF16),
            pltpu.VMEM((n, modes, chan), BF16),
            pltpu.SemaphoreType.DMA((chunks,)),
            pltpu.SemaphoreType.DMA((chunks,)),
            pltpu.SemaphoreType.DMA((chunks,)),
            pltpu.SemaphoreType.DMA((4,)),
            pltpu.SemaphoreType.DMA((n,)),
            pltpu.SemaphoreType.DMA((n,)),
        ],
        compiler_params=pltpu.CompilerParams(
            collective_id=0, has_side_effects=True, vmem_limit_bytes=58 * 1024 * 1024
        ),
        name="mixer",
        cost_estimate=pl.CostEstimate(
            flops=2 * tok * width * 3 * chan, bytes_accessed=2 * width * (tok + 3 * chan), transcendentals=0
        ),
    )(hidden, w_in, norm_gain.reshape(1, width), w_short.T, rates, residues, skip.reshape(1, chan))
    block = min(1024, width)
    return pl.pallas_call(
        project_out,
        out_shape=jax.ShapeDtypeStruct((tok, width), BF16),
        grid=(width // block,),
        in_specs=[vmem, vmem],
        out_specs=pl.BlockSpec((tok, block), lambda j: (0, j)),
        name="project_out",
        compiler_params=pltpu.CompilerParams(vmem_limit_bytes=24 * 1024 * 1024),
        cost_estimate=pl.CostEstimate(
            flops=2 * tok * width * chan, bytes_accessed=2 * width * (tok + chan), transcendentals=0
        ),
    )(gated, w_out)


def solution(mesh):
    return jax.shard_map(
        functools.partial(on_device, mesh.shape["tm"]),
        mesh=mesh,
        in_specs=(P("tm", None), P(), P(), P(), P(), P(), P(), P()),
        out_specs=P("tm", None),
        check_vma=False,
    )
```

profile of v0, /device:TPU:16, one launch (start us, length us, event | category | flops | bytes accessed | tf_op | source)
XLA Modules:
  0.0 27.2 jit_solution(14982933561415452322)
XLA Ops:
  0.0 0.0 copy-start
  0.0 20.9 %mixer.1.gated = bf16[384,256]{1,0:T(8,128)(2,1)} custom-call(bf16[384,8192]{1,0:T(8,128)(2,1)} %hidden.1, bf16[8192,768]{1,0:T(8,128)(2,1)} %w_in.1, f32[1,8192]{1,0:T(1,128)} %bitcast.3, f32[7,768]{1,0:T(8,128)} %bitcast.4, f32[8,16]{1,0:T(8,128)} %rates.1, f32[8,16]{1,0:T(8,128)} %residues.1, f32[1,256]{1,0:T(1,128)} %bitcast.5), custom_call_target="tpu_custom_call" | custom-call | flops 4831838208 | bytes 18874368 | tf_op jit(solution)/shard_map/mixer/pallas_call | solution.py:300
  20.9 0.0 copy-done
  20.9 0.0 copy-start.1
  20.9 0.9 %copy-done.1 = bf16[384,256]{1,0:T(8,128)(2,1)S(1)} copy-done((bf16[384,256]{1,0:T(8,128)(2,1)S(1)}, bf16[384,256]{1,0:T(8,128)(2,1)}, u32[]{:S(2)}) %copy-start.1) | copy-done | bytes 196632
  21.8 5.4 %project_out.1 = bf16[384,8192]{1,0:T(8,128)(2,1)} custom-call(bf16[384,256]{1,0:T(8,128)(2,1)S(1)} %copy-done.1, bf16[256,8192]{1,0:T(8,128)(2,1)S(1)} %copy-done), custom_call_target="tpu_custom_call" | custom-call | flops 1610612736 | bytes 10485760 | tf_op jit(solution)/shard_map/project_out/pallas_call | solution.py:338
Async XLA Ops:
  0.0 20.9 %copy-start = (bf16[256,8192]{1,0:T(8,128)(2,1)S(1)}, bf16[256,8192]{1,0:T(8,128)(2,1)}, u32[]{:S(2)}) copy-start(bf16[256,8192]{1,0:T(8,128)(2,1)} %w_out.1) | copy-start | bytes 12582916
  20.9 0.9 %copy-start.1 = (bf16[384,256]{1,0:T(8,128)(2,1)S(1)}, bf16[384,256]{1,0:T(8,128)(2,1)}, u32[]{:S(2)}) copy-start(bf16[384,256]{1,0:T(8,128)(2,1)} %mixer.1.gated) | copy-start | bytes 589828
where the time goes:
time: 27.3 us; the launch traced here: 27.2 us
  Pallas kernels  26.2 us (96%)
  local copies, waits for them, and re-layouts  0.92 us (3%)
    pallas_call x1, Pallas kernels, on_device(): pl.pallas_call(functools.partial(mixer, n, depth), out_shape=jax.ShapeDty...  20.9 us
    pallas_call x1, Pallas kernels, on_device(): pl.pallas_call(project_out, out_shape=jax.ShapeDtypeStruct((tok, width),...  5.39 us
    unnamed x4, local copies, waits for them, and re-layouts  0.92 us

commit v1 on v0

--- a/solution.py
+++ b/solution.py
@@ -282,10 +282,17 @@
         state_copy(me, d).wait_send()
 
 
-def project_out(gated, w_out, mixed):
-    block = mixed.shape[1]
-    cols = pl.ds(pl.multiple_of(pl.program_id(0) * block, block), block)
-    mixed[...] = dot(gated[...], w_out[:, cols]).astype(BF16)
+def project_out(gated, w_out, mixed, held, sem):
+    parts, _, block = held.shape
+
+    def copy(k):
+        return pltpu.make_async_copy(held.at[k], mixed.at[:, pl.ds(k * block, block)], sem.at[k])
+
+    for k in range(parts):
+        held[k] = dot(gated[...], w_out[:, k * block : (k + 1) * block]).astype(BF16)
+        copy(k).start()
+    for k in range(parts):
+        copy(k).wait()
 
 
 def on_device(n, hidden, norm_gain, w_in, w_short, residues, rates, skip, w_out):
@@ -299,7 +306,7 @@
     in_hbm = pl.BlockSpec(memory_space=pltpu.HBM)
     gated = pl.pallas_call(
         functools.partial(mixer, n, depth),
-        out_shape=jax.ShapeDtypeStruct((tok, chan), BF16),
+        out_shape=pltpu.VMEM((tok, chan), BF16),
         in_specs=[in_hbm, in_hbm] + [vmem] * 5,
         out_specs=vmem,
         scratch_shapes=[
@@ -334,13 +341,16 @@
             flops=2 * tok * width * 3 * chan, bytes_accessed=2 * width * (tok + 3 * chan), transcendentals=0
         ),
     )(hidden, w_in, norm_gain.reshape(1, width), w_short.T, rates, residues, skip.reshape(1, chan))
-    block = min(1024, width)
+    parts = 16
     return pl.pallas_call(
         project_out,
         out_shape=jax.ShapeDtypeStruct((tok, width), BF16),
-        grid=(width // block,),
         in_specs=[vmem, vmem],
-        out_specs=pl.BlockSpec((tok, block), lambda j: (0, j)),
+        out_specs=in_hbm,
+        scratch_shapes=[
+            pltpu.VMEM((parts, tok, width // parts), BF16),
+            pltpu.SemaphoreType.DMA((parts,)),
+        ],
         name="project_out",
         compiler_params=pltpu.CompilerParams(vmem_limit_bytes=24 * 1024 * 1024),
         cost_estimate=pl.CostEstimate(

time: 27.3 us -> 23.4 us (0.86)
  Pallas kernels: 26.2 us -> 23.2 us
  local copies, waits for them, and re-layouts: 0.92 us -> 0.01 us
    pallas_call x1, Pallas kernels: 5.39 us -> 3.05 us  [on_device(): pl.pallas_call(project_out, out_shape=jax.ShapeDtypeStruct((tok, width),...]
    unnamed x4 -> x2, local copies, waits for them, and re-layouts: 0.92 us -> 0.01 us
    pallas_call x1, Pallas kernels: 20.9 us -> 20.2 us  [on_device(): pl.pallas_call(functools.partial(mixer, n, depth), out_shape=pltpu.VMEM((...]
where the time goes in v1:
time: 23.4 us; the launch traced here: 23.3 us
  Pallas kernels  23.2 us (99%)
    pallas_call x1, Pallas kernels, on_device(): pl.pallas_call(functools.partial(mixer, n, depth), out_shape=pltpu.VMEM((...  20.2 us
    pallas_call x1, Pallas kernels, on_device(): pl.pallas_call(project_out, out_shape=jax.ShapeDtypeStruct((tok, width),...  3.05 us

profile of v1, /device:TPU:16, one launch (start us, length us, event | category | flops | bytes accessed | tf_op | source)
XLA Modules:
  0.0 23.3 jit_solution(2148466372735017690)
XLA Ops:
  0.0 0.0 copy-start
  0.0 20.2 %mixer.1.gated = bf16[384,256]{1,0:T(8,128)(2,1)S(1)} custom-call(bf16[384,8192]{1,0:T(8,128)(2,1)} %hidden.1, bf16[8192,768]{1,0:T(8,128)(2,1)} %w_in.1, f32[1,8192]{1,0:T(1,128)} %bitcast.3, f32[7,768]{1,0:T(8,128)} %bitcast.4, f32[8,16]{1,0:T(8,128)} %rates.1, f32[8,16]{1,0:T(8,128)} %residues.1, f32[1,256]{1,0:T(1,128)} %bitcast.5), custom_call_target="tpu_custom_call" | custom-call | flops 4831838208 | bytes 18874368 | tf_op jit(solution)/shard_map/mixer/pallas_call | solution.py:307
  20.2 0.0 copy-done
  20.2 3.1 %project_out.1 = bf16[384,8192]{1,0:T(8,128)(2,1)} custom-call(bf16[384,256]{1,0:T(8,128)(2,1)S(1)} %mixer.1.gated, bf16[256,8192]{1,0:T(8,128)(2,1)S(1)} %copy-done), custom_call_target="tpu_custom_call" | custom-call | flops 1610612736 | bytes 10485760 | tf_op jit(solution)/shard_map/project_out/pallas_call | solution.py:345
Async XLA Ops:
  0.0 20.2 %copy-start = (bf16[256,8192]{1,0:T(8,128)(2,1)S(1)}, bf16[256,8192]{1,0:T(8,128)(2,1)}, u32[]{:S(2)}) copy-start(bf16[256,8192]{1,0:T(8,128)(2,1)} %w_out.1) | copy-start | bytes 12582916

commit v2 on v1

--- a/solution.py
+++ b/solution.py
@@ -29,10 +29,11 @@
 
 
 def mixer(
-    n, depth, hidden, w_in, gain, taps, rates, residues, skip, out,
+    n, depth, hidden, w_in, w_out, gain_far, taps_far, rates_far, residues_far, skip_far, out, w_out_near,
+    gain, taps, rates, residues, skip,
     held, w_kv, w_q, acc_kv, acc_q, squares, proj_kv, proj_q, prod, feat_q,
     fall, rise, lag_row, toeplitz, own, slots,
-    held_sem, kv_sem, q_sem, edge_sem, send_sem, recv_sem,
+    held_sem, kv_sem, q_sem, edge_sem, send_sem, recv_sem, out_sem, small_sem,
 ):
     me = lax.axis_index("tm")
     following = lax.rem(me + 1, n)
@@ -43,11 +44,14 @@
     per_group = chan // groups
     chunks = width // depth
 
-    barrier = pltpu.get_barrier_semaphore()
-
-    @pl.loop(0, me)
-    def _(d):
-        pl.semaphore_signal(barrier, inc=1, device_id=(d,), device_id_type=MESH)
+    small = [
+        pltpu.make_async_copy(source, target, small_sem.at[i])
+        for i, (source, target) in enumerate(
+            [(rates_far, rates), (residues_far, residues), (gain_far, gain), (taps_far, taps), (skip_far, skip)]
+        )
+    ]
+    for copy in small:
+        copy.start()
 
     def held_copy(k):
         cols = pl.ds(pl.multiple_of(k * depth, depth), depth)
@@ -68,7 +72,19 @@
 
     @pl.loop(0, chunks)
     def _(k):
-        q_copy(k).start()
+        q_copy(k).start(priority=1)
+
+    out_copy = pltpu.make_async_copy(w_out, w_out_near, out_sem)
+    out_copy.start(priority=1)
+
+    barrier = pltpu.get_barrier_semaphore()
+
+    @pl.loop(0, me)
+    def _(d):
+        pl.semaphore_signal(barrier, inc=1, device_id=(d,), device_id_type=MESH)
+
+    for copy in small:
+        copy.wait()
 
     pick = (iota((modes, every), 1) % modes == iota((modes, every), 0)).astype(F32)
     mine = iota((groups, every), 1) // modes == iota((groups, every), 0)
@@ -147,9 +163,6 @@
     def _():
         edge_copy(proj_kv, 0).start()
 
-    half = chunks // 2
-    strip = tok // half
-
     def feature(buf, r, rows, first, tap_first):
         total = jnp.zeros((rows, chan), F32)
         for t in range(taps.shape[0]):
@@ -158,47 +171,43 @@
             ]
         return total
 
-    def query_step(k, start):
+    def key_value(r):
+        keyed = feature(proj_kv, r, 32, 0, chan)
+        valued = feature(proj_kv, r, 32, chan, 2 * chan)
+        prod[pl.ds(r, 32)] = (keyed * valued).astype(BF16)
+
+    def query_step(k):
         q_copy(k).wait()
-        for r in range(0, strip, 32):
-            keyed = feature(proj_kv, start + r, 32, 0, chan)
-            valued = feature(proj_kv, start + r, 32, chan, 2 * chan)
-            prod[pl.ds(start + r, 32)] = (keyed * valued).astype(BF16)
         acc_q[...] += dot(held[k], w_q[k])
 
     tiles = tok // LANES
     causal = iota((LANES, LANES), 0) >= iota((LANES, LANES), 1)
-    share = groups // (chunks - half)
-
-    def toeplitz_step(k):
-        q_copy(k).wait()
-        for e in range(share):
-            g = (k - half) * share + e
-            first = jnp.broadcast_to(lag_row[pl.ds(g, 1)], (LANES, tok))
-            moved = pltpu.roll(first, 0, 1, stride=1, stride_axis=0)
-            lags = []
-            for i in range(tiles):
-                at = (tiles - i) % tiles * LANES
-                tile = moved[:, at : at + LANES]
-                lags.append((jnp.where(causal, tile, 0.0) if i == 0 else tile).astype(BF16))
-            for i in range(tiles):
-                for j in range(tiles):
-                    value = lags[i - j] if i >= j else jnp.zeros((LANES, LANES), BF16)
-                    toeplitz[g, i * LANES : (i + 1) * LANES, j * LANES : (j + 1) * LANES] = value
-        acc_q[...] += dot(held[k], w_q[k])
-
-    for k in range(1, half):
-        query_step(k, k * strip)
-
-    early = half + (chunks - half) // 2
-
-    pl.loop(half, early)(toeplitz_step)
+    def toeplitz_step(g):
+        first = jnp.broadcast_to(lag_row[pl.ds(g, 1)], (LANES, tok))
+        moved = pltpu.roll(first, 0, 1, stride=1, stride_axis=0)
+        lags = []
+        for i in range(tiles):
+            at = (tiles - i) % tiles * LANES
+            tile = moved[:, at : at + LANES]
+            lags.append((jnp.where(causal, tile, 0.0) if i == 0 else tile).astype(BF16))
+        for i in range(tiles):
+            for j in range(tiles):
+                value = lags[i - j] if i >= j else jnp.zeros((LANES, LANES), BF16)
+                toeplitz[g, i * LANES : (i + 1) * LANES, j * LANES : (j + 1) * LANES] = value
+
+    for r in range(32, tok, 32):
+        key_value(r)
+
+    pl.loop(0, groups)(toeplitz_step)
+
+    early = chunks // 2
+    pl.loop(0, early)(query_step)
 
     @pl.when(me > 0)
     def _():
         edge_copy(proj_kv, 0).wait_recv()
 
-    query_step(0, 0)
+    key_value(0)
 
     both = dot(fall[...], prod[...])
     wide = both[:every] + both[every:]
@@ -219,7 +228,7 @@
     def _(d):
         state_copy(me, d).start()
 
-    pl.loop(early, chunks)(toeplitz_step)
+    pl.loop(early, chunks)(query_step)
 
     proj_q[EDGE:] = acc_q[...] * inv
 
@@ -272,6 +281,8 @@
     far = dot(rise[...], jnp.concatenate([high, high], axis=0)) + dot(rise[:, :every], low)
     out[...] = (feat_q[...] * (acc_q[...] + far)).astype(BF16)
 
+    out_copy.wait()
+
     @pl.when(me < n - 1)
     def _():
         edge_copy(proj_kv, 0).wait_send()
@@ -304,12 +315,17 @@
     chunks = width // depth
     vmem = pl.BlockSpec(memory_space=pltpu.VMEM)
     in_hbm = pl.BlockSpec(memory_space=pltpu.HBM)
-    gated = pl.pallas_call(
+    gated, w_out_near = pl.pallas_call(
         functools.partial(mixer, n, depth),
-        out_shape=pltpu.VMEM((tok, chan), BF16),
-        in_specs=[in_hbm, in_hbm] + [vmem] * 5,
-        out_specs=vmem,
+        out_shape=[pltpu.VMEM((tok, chan), BF16), pltpu.VMEM((chan, width), BF16)],
+        in_specs=[in_hbm] * 8,
+        out_specs=[vmem, vmem],
         scratch_shapes=[
+            pltpu.VMEM((1, width), F32),
+            pltpu.VMEM((w_short.shape[1], 3 * chan), F32),
+            pltpu.VMEM((groups, modes), F32),
+            pltpu.VMEM((groups, modes), F32),
+            pltpu.VMEM((1, chan), F32),
             pltpu.VMEM((chunks, tok, depth), BF16),
             pltpu.VMEM((chunks, depth, 2 * chan), BF16),
             pltpu.VMEM((chunks, depth, chan), BF16),
@@ -332,15 +348,23 @@
             pltpu.SemaphoreType.DMA((4,)),
             pltpu.SemaphoreType.DMA((n,)),
             pltpu.SemaphoreType.DMA((n,)),
+            pltpu.SemaphoreType.DMA,
+            pltpu.SemaphoreType.DMA((5,)),
         ],
         compiler_params=pltpu.CompilerParams(
-            collective_id=0, has_side_effects=True, vmem_limit_bytes=58 * 1024 * 1024
+            collective_id=0, has_side_effects=True, vmem_limit_bytes=48 * 1024 * 1024
         ),
         name="mixer",
         cost_estimate=pl.CostEstimate(
             flops=2 * tok * width * 3 * chan, bytes_accessed=2 * width * (tok + 3 * chan), transcendentals=0
         ),
-    )(hidden, w_in, norm_gain.reshape(1, width), w_short.T, rates, residues, skip.reshape(1, chan))
+    )(
+        hidden, w_in, w_out,
+        *(
+            pltpu.with_memory_space_constraint(x, pltpu.HBM)
+            for x in (norm_gain.reshape(1, width), w_short.T, rates, residues, skip.reshape(1, chan))
+        ),
+    )
     parts = 16
     return pl.pallas_call(
         project_out,
@@ -356,7 +380,7 @@
         cost_estimate=pl.CostEstimate(
             flops=2 * tok * width * chan, bytes_accessed=2 * width * (tok + chan), transcendentals=0
         ),
-    )(gated, w_out)
+    )(gated, w_out_near)
 
 
 def solution(mesh):

time: 23.4 us -> 22.7 us (0.970)
  Pallas kernels: 23.2 us -> 22.5 us
    pallas_call x1, Pallas kernels: 20.2 us -> 19.4 us  [on_device(): pl.pallas_call(functools.partial(mixer, n, depth), out_shape=[pltpu.VMEM(...]
where the time goes in v2:
time: 22.7 us; the launch traced here: 22.5 us
  Pallas kernels  22.5 us (99%)
    pallas_call x1, Pallas kernels, on_device(): pl.pallas_call(functools.partial(mixer, n, depth), out_shape=[pltpu.VMEM(...  19.4 us
    pallas_call x1, Pallas kernels, on_device(): pl.pallas_call(project_out, out_shape=jax.ShapeDtypeStruct((tok, width),...  3.05 us

profile of v2, /device:TPU:16, one launch (start us, length us, event | category | flops | bytes accessed | tf_op | source)
XLA Modules:
  0.0 22.5 jit_solution(16003307292323471584)
XLA Ops:
  0.0 19.4 %mixer.1 = (bf16[384,256]{1,0:T(8,128)(2,1)S(1)}, bf16[256,8192]{1,0:T(8,128)(2,1)S(1)}) custom-call(bf16[384,8192]{1,0:T(8,128)(2,1)} %hidden.1, bf16[8192,768]{1,0:T(8,128)(2,1)} %w_in.1, bf16[256,8192]{1,0:T(8,128)(2,1)} %w_out.1, f32[1,8192]{1,0:T(1,128)} %bitcast.3, f32[7,768]{1,0:T(8,128)} %bitcast.4, f32[8,16]{1,0:T(8,128)} %rates_far.1, ...), custom_call_target="tpu_custom_call" | custom-call | flops 4831838208 | bytes 18874368 | tf_op jit(solution)/shard_map/mixer/pallas_call | solution.py:318
  19.4 3.1 %project_out.1 = bf16[384,8192]{1,0:T(8,128)(2,1)} custom-call(bf16[384,256]{1,0:T(8,128)(2,1)S(1)} %get-tuple-element.7.gated, bf16[256,8192]{1,0:T(8,128)(2,1)S(1)} %get-tuple-element.8.w_out), custom_call_target="tpu_custom_call" | custom-call | flops 1610612736 | bytes 10485760 | tf_op jit(solution)/shard_map/project_out/pallas_call | solution.py:369

commit v3 on v2

--- a/solution.py
+++ b/solution.py
@@ -32,11 +32,14 @@
     n, depth, hidden, w_in, w_out, gain_far, taps_far, rates_far, residues_far, skip_far, out, w_out_near,
     gain, taps, rates, residues, skip,
     held, w_kv, w_q, acc_kv, acc_q, squares, proj_kv, proj_q, prod, feat_q,
-    fall, rise, lag_row, toeplitz, own, slots,
-    held_sem, kv_sem, q_sem, edge_sem, send_sem, recv_sem, out_sem, small_sem,
+    fall, rise, lag_row, toeplitz, lead, other_lead, edge_fall, mine_state, other_state, even_state, own, slots,
+    held_sem, kv_sem, q_sem, near_send, near_recv, send_sem, recv_sem, out_sem, small_sem,
 ):
     me = lax.axis_index("tm")
     following = lax.rem(me + 1, n)
+    pairs = n // 2
+    pair, side = me // 2, lax.rem(me, 2)
+    sibling = me + 1 - 2 * side
     tok, width = hidden.shape
     chan = prod.shape[1]
     groups, modes = rates.shape
@@ -79,9 +82,18 @@
 
     barrier = pltpu.get_barrier_semaphore()
 
-    @pl.loop(0, me)
-    def _(d):
+    def greet(d):
         pl.semaphore_signal(barrier, inc=1, device_id=(d,), device_id_type=MESH)
+
+    @pl.loop(0, pair)
+    def _(p):
+        greet(2 * p + side)
+
+    greet(sibling)
+
+    @pl.when(jnp.logical_and(side == 0, pair > 0))
+    def _():
+        greet(me - 1)
 
     for copy in small:
         copy.wait()
@@ -110,7 +122,11 @@
     rate_mc = by_channel(rates[...])
     weight_mc = by_channel(weights)
     high, low = split(jnp.exp(-rate_col * (tok - 1 - iota((every, tok), 1)).astype(F32)))
-    fall[:every], fall[every:] = high, low
+    early_rows = iota((every, tok), 1) < EDGE
+    fall[:every] = jnp.where(early_rows, jnp.zeros_like(high), high)
+    fall[every:] = jnp.where(early_rows, jnp.zeros_like(low), low)
+    for r in range(EDGE):
+        edge_fall[r] = jnp.exp(-rate_mc * float(tok - 1 - r))
     high, low = split(jnp.exp(-rate_row * (iota((tok, every), 0) + 1).astype(F32)))
     rise[:, :every], rise[:, every:] = high, low
     back = lax.rem(tok - iota((every, tok), 1), tok).astype(F32)
@@ -118,6 +134,7 @@
     for g in range(groups):
         lag_row[g : g + 1] = jnp.sum(terms[g * modes : (g + 1) * modes], axis=0, keepdims=True)
 
+    even_state[...] = jnp.zeros_like(even_state)
     acc_kv[...] = jnp.zeros_like(acc_kv)
     acc_q[...] = jnp.zeros_like(acc_q)
     squares[...] = jnp.zeros_like(squares)
@@ -141,40 +158,66 @@
         acc_kv[...] += dot(scaled, w_kv[k])
 
     inv = lax.rsqrt(jnp.sum(squares[...], axis=1, keepdims=True) / width + 1e-06)
-    proj_kv[EDGE:] = acc_kv[...] * inv
+    proj_kv[...] = acc_kv[...] * inv
+    pl.semaphore_wait(barrier, pairs - pair + side * jnp.minimum(pairs - 1 - pair, 1))
+
+    def near_copy(i, source, target, device):
+        return pltpu.make_async_remote_copy(
+            src_ref=source, dst_ref=target, send_sem=near_send.at[i], recv_sem=near_recv.at[i],
+            device_id=(device,), device_id_type=MESH,
+        )
+
+    before, first = pl.ds(0, EDGE), pl.ds(EDGE, EDGE)
+    last = proj_kv.at[pl.ds(tok - EDGE, EDGE)]
+    halo = near_copy(0, last, lead.at[before], following)
+    far_halo = near_copy(1, last, other_lead.at[before], lax.rem(me + 2, n))
+    heading = near_copy(2, proj_kv.at[before], other_lead.at[first], sibling)
+    swap = near_copy(3, mine_state, other_state, sibling)
+    q_halo = near_copy(4, proj_q.at[pl.ds(tok, EDGE)], proj_q.at[before], following)
+    has_next = me < n - 1
+    sends_far = jnp.logical_and(side == 1, has_next)
+
+    @pl.when(has_next)
+    def _():
+        halo.start()
+
+    @pl.when(sends_far)
+    def _():
+        far_halo.start()
+
+    @pl.when(side == 0)
+    def _():
+        heading.start()
+
+    lead[EDGE:] = proj_kv[:EDGE]
 
     @pl.when(me == 0)
     def _():
-        proj_kv[:EDGE] = jnp.zeros((EDGE, 2 * chan), F32)
+        lead[:EDGE] = jnp.zeros((EDGE, 2 * chan), F32)
         proj_q[:EDGE] = jnp.zeros((EDGE, chan), F32)
 
-    @pl.when(me < n - 1)
-    def _():
-        pl.semaphore_wait(barrier, n - 1 - me)
-
-    def edge_copy(buf, i):
-        return pltpu.make_async_remote_copy(
-            src_ref=buf.at[pl.ds(tok, EDGE)], dst_ref=buf.at[pl.ds(0, EDGE)],
-            send_sem=edge_sem.at[2 * i], recv_sem=edge_sem.at[2 * i + 1],
-            device_id=(following,), device_id_type=MESH,
-        )
-
-    @pl.when(me < n - 1)
-    def _():
-        edge_copy(proj_kv, 0).start()
+    @pl.when(me == 1)
+    def _():
+        other_lead[:EDGE] = jnp.zeros((EDGE, 2 * chan), F32)
 
     def feature(buf, r, rows, first, tap_first):
         total = jnp.zeros((rows, chan), F32)
         for t in range(taps.shape[0]):
             total = total + taps[t : t + 1, tap_first : tap_first + chan] * buf[
-                pl.ds(r + EDGE - t, rows), first : first + chan
+                pl.ds(r - t, rows), first : first + chan
             ]
         return total
 
-    def key_value(r):
-        keyed = feature(proj_kv, r, 32, 0, chan)
-        valued = feature(proj_kv, r, 32, chan, 2 * chan)
-        prod[pl.ds(r, 32)] = (keyed * valued).astype(BF16)
+    def key_value(buf, r, rows):
+        keyed = feature(buf, r, rows, 0, chan)
+        valued = feature(buf, r, rows, chan, 2 * chan)
+        return (keyed * valued).astype(BF16)
+
+    def edge_state(product):
+        total = jnp.zeros((modes, chan), F32)
+        for r in range(EDGE):
+            total = total + edge_fall[r] * product[r : r + 1].astype(F32)
+        return total
 
     def query_step(k):
         q_copy(k).wait()
@@ -195,19 +238,10 @@
                 value = lags[i - j] if i >= j else jnp.zeros((LANES, LANES), BF16)
                 toeplitz[g, i * LANES : (i + 1) * LANES, j * LANES : (j + 1) * LANES] = value
 
+    zeros = jnp.zeros((EDGE, chan), BF16)
+    prod[:32] = jnp.concatenate([zeros, key_value(proj_kv, EDGE, 32 - EDGE)], axis=0)
     for r in range(32, tok, 32):
-        key_value(r)
-
-    pl.loop(0, groups)(toeplitz_step)
-
-    early = chunks // 2
-    pl.loop(0, early)(query_step)
-
-    @pl.when(me > 0)
-    def _():
-        edge_copy(proj_kv, 0).wait_recv()
-
-    key_value(0)
+        prod[r : r + 32] = key_value(proj_kv, r, 32)
 
     both = dot(fall[...], prod[...])
     wide = both[:every] + both[every:]
@@ -215,26 +249,70 @@
     packed = jnp.zeros((modes, chan), F32)
     for g in range(groups):
         packed = packed + jnp.where(group_of == g, wide[g * modes : (g + 1) * modes], 0.0)
-    own[...] = packed.astype(BF16)
+
+    @pl.when(side == 0)
+    def _():
+        mine_state[...] = packed
+        swap.start()
+
+    pl.loop(0, groups // 2)(toeplitz_step)
+
+    @pl.when(side == 1)
+    def _():
+        halo.wait_recv()
+        rows = key_value(lead, EDGE, EDGE)
+        prod[:EDGE] = rows
+        mine_state[...] = packed + edge_state(rows)
+        swap.start()
+
+    pl.loop(groups // 2, groups)(toeplitz_step)
+
+    early = chunks // 2
+    pl.loop(0, early)(query_step)
+    decay = jnp.exp(-rate_mc * float(tok))
+
+    @pl.when(jnp.logical_and(side == 0, me > 0))
+    def _():
+        halo.wait_recv()
+
+    @pl.when(side == 0)
+    def _():
+        rows = key_value(lead, EDGE, EDGE)
+        prod[:EDGE] = rows
+        whole = packed + edge_state(rows)
+        swap.wait_recv()
+        own[...] = (decay * whole + other_state[...]).astype(BF16)
+
+    @pl.when(jnp.logical_and(side == 1, pair > 0))
+    def _():
+        far_halo.wait_recv()
+
+    @pl.when(side == 1)
+    def _():
+        heading.wait_recv()
+        swap.wait_recv()
+        whole = other_state[...] + edge_state(key_value(other_lead, EDGE, EDGE))
+        even_state[...] = whole
+        own[...] = (decay * whole + mine_state[...]).astype(BF16)
 
     def state_copy(source, target):
         return pltpu.make_async_remote_copy(
             src_ref=own, dst_ref=slots.at[source],
             send_sem=send_sem.at[target], recv_sem=recv_sem.at[source],
-            device_id=(target,), device_id_type=MESH,
+            device_id=(2 * target + side,), device_id_type=MESH,
         )
 
-    @pl.loop(me + 1, n)
-    def _(d):
-        state_copy(me, d).start()
+    @pl.loop(0, pairs - 1 - pair)
+    def _(i):
+        state_copy(pair, pairs - 1 - i).start()
 
     pl.loop(early, chunks)(query_step)
 
     proj_q[EDGE:] = acc_q[...] * inv
 
-    @pl.when(me < n - 1)
-    def _():
-        edge_copy(proj_q, 1).start()
+    @pl.when(has_next)
+    def _():
+        q_halo.start()
 
     product = prod[...]
     channel_group = iota((tok, chan), 1) // per_group
@@ -260,21 +338,22 @@
     add(convolve(range(groups // 2)))
 
     for r in range(32, tok, 32):
-        feat_q[r : r + 32] = feature(proj_q, r, 32, 0, 0)
+        feat_q[r : r + 32] = feature(proj_q, EDGE + r, 32, 0, 0)
     add(convolve(range(groups // 2, groups)))
 
-    decay = jnp.exp(-rate_mc * float(tok))
-
-    def gather(d, state):
-        state_copy(d, following).wait_recv()
-        return decay * state + slots[d].astype(F32)
+    pair_decay = jnp.exp(-rate_mc * float(2 * tok))
+
+    def gather(p, state):
+        state_copy(p, pair).wait_recv()
+        return pair_decay * state + slots[p].astype(F32)
 
     @pl.when(me > 0)
     def _():
-        edge_copy(proj_q, 1).wait_recv()
-
-    feat_q[:32] = feature(proj_q, 0, 32, 0, 0)
-    state = lax.fori_loop(0, me, gather, jnp.zeros((modes, chan), F32)) * weight_mc
+        q_halo.wait_recv()
+
+    feat_q[:32] = feature(proj_q, EDGE, 32, 0, 0)
+    state = lax.fori_loop(0, pair, gather, jnp.zeros((modes, chan), F32))
+    state = jnp.where(side == 1, decay * state + even_state[...], state) * weight_mc
     stacked = jnp.concatenate([state] * groups, axis=0)
     same = iota((every, chan), 0) // modes == iota((every, chan), 1) // per_group
     high, low = split(jnp.where(same, stacked, 0.0))
@@ -283,14 +362,24 @@
 
     out_copy.wait()
 
-    @pl.when(me < n - 1)
-    def _():
-        edge_copy(proj_kv, 0).wait_send()
-        edge_copy(proj_q, 1).wait_send()
-
-    @pl.loop(me + 1, n)
-    def _(d):
-        state_copy(me, d).wait_send()
+    swap.wait_send()
+
+    @pl.when(has_next)
+    def _():
+        halo.wait_send()
+        q_halo.wait_send()
+
+    @pl.when(sends_far)
+    def _():
+        far_halo.wait_send()
+
+    @pl.when(side == 0)
+    def _():
+        heading.wait_send()
+
+    @pl.loop(pair + 1, pairs)
+    def _(p):
+        state_copy(pair, p).wait_send()
 
 
 def project_out(gated, w_out, mixed, held, sem):
@@ -332,7 +421,7 @@
             pltpu.VMEM((tok, 2 * chan), F32),
             pltpu.VMEM((tok, chan), F32),
             pltpu.VMEM((tok, LANES), F32),
-            pltpu.VMEM((EDGE + tok, 2 * chan), F32),
+            pltpu.VMEM((tok, 2 * chan), F32),
             pltpu.VMEM((EDGE + tok, chan), F32),
             pltpu.VMEM((tok, chan), BF16),
             pltpu.VMEM((tok, chan), F32),
@@ -340,14 +429,21 @@
             pltpu.VMEM((tok, 2 * every), BF16),
             pltpu.VMEM((groups, tok), F32),
             pltpu.VMEM((groups, tok, tok), BF16),
+            pltpu.VMEM((2 * EDGE, 2 * chan), F32),
+            pltpu.VMEM((2 * EDGE, 2 * chan), F32),
+            pltpu.VMEM((EDGE, modes, chan), F32),
+            pltpu.VMEM((modes, chan), F32),
+            pltpu.VMEM((modes, chan), F32),
+            pltpu.VMEM((modes, chan), F32),
             pltpu.VMEM((modes, chan), BF16),
-            pltpu.VMEM((n, modes, chan), BF16),
+            pltpu.VMEM((n // 2, modes, chan), BF16),
             pltpu.SemaphoreType.DMA((chunks,)),
             pltpu.SemaphoreType.DMA((chunks,)),
             pltpu.SemaphoreType.DMA((chunks,)),
-            pltpu.SemaphoreType.DMA((4,)),
-            pltpu.SemaphoreType.DMA((n,)),
-            pltpu.SemaphoreType.DMA((n,)),
+            pltpu.SemaphoreType.DMA((5,)),
+            pltpu.SemaphoreType.DMA((5,)),
+            pltpu.SemaphoreType.DMA((n // 2,)),
+            pltpu.SemaphoreType.DMA((n // 2,)),
             pltpu.SemaphoreType.DMA,
             pltpu.SemaphoreType.DMA((5,)),
         ],

time: 22.7 us -> 20 us (0.88)
  Pallas kernels: 22.5 us -> 19.8 us
    pallas_call x1, Pallas kernels: 19.4 us -> 16.7 us  [on_device(): pl.pallas_call(functools.partial(mixer, n, depth), out_shape=[pltpu.VMEM(...]
where the time goes in v3:
time: 20 us; the launch traced here: 19.8 us
  Pallas kernels  19.8 us (99%)
    pallas_call x1, Pallas kernels, on_device(): pl.pallas_call(functools.partial(mixer, n, depth), out_shape=[pltpu.VMEM(...  16.7 us
    pallas_call x1, Pallas kernels, on_device(): pl.pallas_call(project_out, out_shape=jax.ShapeDtypeStruct((tok, width),...  3.05 us

profile of v3, /device:TPU:16, one launch (start us, length us, event | category | flops | bytes accessed | tf_op | source)
XLA Modules:
  0.0 19.8 jit_solution(11496491240986037052)
XLA Ops:
  0.0 16.7 %mixer.1 = (bf16[384,256]{1,0:T(8,128)(2,1)S(1)}, bf16[256,8192]{1,0:T(8,128)(2,1)S(1)}) custom-call(bf16[384,8192]{1,0:T(8,128)(2,1)} %hidden.1, bf16[8192,768]{1,0:T(8,128)(2,1)} %w_in.1, bf16[256,8192]{1,0:T(8,128)(2,1)} %w_out.1, f32[1,8192]{1,0:T(1,128)} %bitcast.3, f32[7,768]{1,0:T(8,128)} %bitcast.4, f32[8,16]{1,0:T(8,128)} %rates_far.1, ...), custom_call_target="tpu_custom_call" | custom-call | flops 4831838208 | bytes 18874368 | tf_op jit(solution)/shard_map/mixer/pallas_call | solution.py:407
  16.7 3.1 %project_out.1 = bf16[384,8192]{1,0:T(8,128)(2,1)} custom-call(bf16[384,256]{1,0:T(8,128)(2,1)S(1)} %get-tuple-element.7.gated, bf16[256,8192]{1,0:T(8,128)(2,1)S(1)} %get-tuple-element.8.w_out), custom_call_target="tpu_custom_call" | custom-call | flops 1610612736 | bytes 10485760 | tf_op jit(solution)/shard_map/project_out/pallas_call | solution.py:465

commit v4 on v3

--- a/solution.py
+++ b/solution.py
@@ -11,6 +11,7 @@
 MESH = pl.DeviceIdType.MESH
 LANES = 128
 EDGE = 8
+TAIL = 16
 F32 = jnp.float32
 BF16 = jnp.bfloat16
 
@@ -33,7 +34,7 @@
     gain, taps, rates, residues, skip,
     held, w_kv, w_q, acc_kv, acc_q, squares, proj_kv, proj_q, prod, feat_q,
     fall, rise, lag_row, toeplitz, lead, other_lead, edge_fall, mine_state, other_state, even_state, own, slots,
-    held_sem, kv_sem, q_sem, near_send, near_recv, send_sem, recv_sem, out_sem, small_sem,
+    held_sem, kv_sem, q_sem, tail_sem, near_send, near_recv, send_sem, recv_sem, out_sem, small_sem,
 ):
     me = lax.axis_index("tm")
     following = lax.rem(me + 1, n)
@@ -56,9 +57,20 @@
     for copy in small:
         copy.start()
 
+    late = chunks // 2
+    body = tok - TAIL
+
     def held_copy(k):
         cols = pl.ds(pl.multiple_of(k * depth, depth), depth)
-        return pltpu.make_async_copy(hidden.at[:, cols], held.at[k], held_sem.at[k])
+        if k < late:
+            return pltpu.make_async_copy(hidden.at[:, cols], held.at[k], held_sem.at[k])
+        rows = pl.ds(0, body)
+        return pltpu.make_async_copy(hidden.at[rows, cols], held.at[k, rows], held_sem.at[k])
+
+    def tail_copy(k):
+        cols = pl.ds(pl.multiple_of(k * depth, depth), depth)
+        rows = pl.ds(body, TAIL)
+        return pltpu.make_async_copy(hidden.at[rows, cols], held.at[k, rows], tail_sem.at[k])
 
     def kv_copy(k):
         rows = pl.ds(pl.multiple_of(k * depth, depth), depth)
@@ -68,10 +80,11 @@
         rows = pl.ds(pl.multiple_of(k * depth, depth), depth)
         return pltpu.make_async_copy(w_in.at[rows, pl.ds(0, chan)], w_q.at[k], q_sem.at[k])
 
-    @pl.loop(0, chunks)
-    def _(k):
+    for k in range(chunks):
+        kv_copy(k).start()
+        (held_copy if k < late else tail_copy)(k).start()
+    for k in range(late, chunks):
         held_copy(k).start()
-        kv_copy(k).start()
 
     @pl.loop(0, chunks)
     def _(k):
@@ -121,44 +134,84 @@
     weight_col = as_column(as_row(weights))
     rate_mc = by_channel(rates[...])
     weight_mc = by_channel(weights)
-    high, low = split(jnp.exp(-rate_col * (tok - 1 - iota((every, tok), 1)).astype(F32)))
-    early_rows = iota((every, tok), 1) < EDGE
-    fall[:every] = jnp.where(early_rows, jnp.zeros_like(high), high)
-    fall[every:] = jnp.where(early_rows, jnp.zeros_like(low), low)
-    for r in range(EDGE):
-        edge_fall[r] = jnp.exp(-rate_mc * float(tok - 1 - r))
-    high, low = split(jnp.exp(-rate_row * (iota((tok, every), 0) + 1).astype(F32)))
-    rise[:, :every], rise[:, every:] = high, low
-    back = lax.rem(tok - iota((every, tok), 1), tok).astype(F32)
-    terms = weight_col * jnp.exp(-rate_col * back)
-    for g in range(groups):
-        lag_row[g : g + 1] = jnp.sum(terms[g * modes : (g + 1) * modes], axis=0, keepdims=True)
+    tiles = tok // LANES
+    causal = iota((LANES, LANES), 0) >= iota((LANES, LANES), 1)
+
+    def make_fall():
+        high, low = split(jnp.exp(-rate_col * (tok - 1 - iota((every, tok), 1)).astype(F32)))
+        early_rows = iota((every, tok), 1) < EDGE
+        fall[:every] = jnp.where(early_rows, jnp.zeros_like(high), high)
+        fall[every:] = jnp.where(early_rows, jnp.zeros_like(low), low)
+
+    def make_rise():
+        high, low = split(jnp.exp(-rate_row * (iota((tok, every), 0) + 1).astype(F32)))
+        rise[:, :every], rise[:, every:] = high, low
+
+    def make_lags():
+        for r in range(EDGE):
+            edge_fall[r] = jnp.exp(-rate_mc * float(tok - 1 - r))
+        back = lax.rem(tok - iota((every, tok), 1), tok).astype(F32)
+        terms = weight_col * jnp.exp(-rate_col * back)
+        for g in range(groups):
+            lag_row[g : g + 1] = jnp.sum(terms[g * modes : (g + 1) * modes], axis=0, keepdims=True)
+
+    def make_toeplitz(some):
+        for g in some:
+            top = jnp.broadcast_to(lag_row[g : g + 1], (LANES, tok))
+            moved = pltpu.roll(top, 0, 1, stride=1, stride_axis=0)
+            lags = []
+            for i in range(tiles):
+                at = (tiles - i) % tiles * LANES
+                tile = moved[:, at : at + LANES]
+                lags.append((jnp.where(causal, tile, 0.0) if i == 0 else tile).astype(BF16))
+            for i in range(tiles):
+                for j in range(tiles):
+                    value = lags[i - j] if i >= j else jnp.zeros((LANES, LANES), BF16)
+                    toeplitz[g, i * LANES : (i + 1) * LANES, j * LANES : (j + 1) * LANES] = value
 
     even_state[...] = jnp.zeros_like(even_state)
-    acc_kv[...] = jnp.zeros_like(acc_kv)
-    acc_q[...] = jnp.zeros_like(acc_q)
-    squares[...] = jnp.zeros_like(squares)
-
-    @pl.loop(0, chunks)
-    def _(k):
-        held_copy(k).wait()
-        kv_copy(k).wait()
-        scale = gain[:, pl.ds(pl.multiple_of(k * depth, depth), depth)]
+
+    def ingest(k, first, stop):
+        scale = gain[:, k * depth : (k + 1) * depth]
         parts = []
-        for r in range(0, tok, 16):
+        for r in range(first, stop, 16):
             x = held[k, r : r + 16].astype(F32)
             sq = x * x
-            total = squares[r : r + 16]
-            for j in range(0, depth, LANES):
+            total = sq[:, :LANES] if k == 0 else squares[r : r + 16] + sq[:, :LANES]
+            for j in range(LANES, depth, LANES):
                 total = total + sq[:, j : j + LANES]
             squares[r : r + 16] = total
             parts.append((x * scale).astype(BF16))
         scaled = jnp.concatenate(parts, axis=0)
-        held[k] = scaled
-        acc_kv[...] += dot(scaled, w_kv[k])
-
-    inv = lax.rsqrt(jnp.sum(squares[...], axis=1, keepdims=True) / width + 1e-06)
-    proj_kv[...] = acc_kv[...] * inv
+        held[k, first:stop] = scaled
+        if k == 0:
+            acc_kv[first:stop] = dot(scaled, w_kv[k])
+        else:
+            acc_kv[first:stop] += dot(scaled, w_kv[k])
+
+    jobs = [make_lags, make_fall] + [functools.partial(make_toeplitz, [g]) for g in range(groups)]
+    where = [k for k in range(chunks) if 0 < k < chunks - 1] or [0]
+
+    def beside(k):
+        for i, job in enumerate(jobs):
+            if where[i * len(where) // len(jobs)] == k:
+                job()
+
+    for k in range(late):
+        held_copy(k).wait()
+        kv_copy(k).wait()
+        ingest(k, 0, tok)
+        beside(k)
+    for k in range(late, chunks):
+        kv_copy(k).wait()
+        tail_copy(k).wait()
+        ingest(k, body, tok)
+
+    def inverse(rows):
+        return lax.rsqrt(jnp.sum(squares[rows], axis=1, keepdims=True) / width + 1e-06)
+
+    tail_inv = inverse(slice(body, tok))
+    proj_kv[body:] = acc_kv[body:] * tail_inv
     pl.semaphore_wait(barrier, pairs - pair + side * jnp.minimum(pairs - 1 - pair, 1))
 
     def near_copy(i, source, target, device):
@@ -185,6 +238,14 @@
     def _():
         far_halo.start()
 
+    for k in range(late, chunks):
+        held_copy(k).wait()
+        ingest(k, 0, body)
+        beside(k)
+
+    inv = jnp.concatenate([inverse(slice(0, body)), tail_inv], axis=0)
+    proj_kv[:body] = acc_kv[:body] * inv[:body]
+
     @pl.when(side == 0)
     def _():
         heading.start()
@@ -219,32 +280,24 @@
             total = total + edge_fall[r] * product[r : r + 1].astype(F32)
         return total
 
-    def query_step(k):
-        q_copy(k).wait()
-        acc_q[...] += dot(held[k], w_q[k])
-
-    tiles = tok // LANES
-    causal = iota((LANES, LANES), 0) >= iota((LANES, LANES), 1)
-    def toeplitz_step(g):
-        first = jnp.broadcast_to(lag_row[pl.ds(g, 1)], (LANES, tok))
-        moved = pltpu.roll(first, 0, 1, stride=1, stride_axis=0)
-        lags = []
-        for i in range(tiles):
-            at = (tiles - i) % tiles * LANES
-            tile = moved[:, at : at + LANES]
-            lags.append((jnp.where(causal, tile, 0.0) if i == 0 else tile).astype(BF16))
-        for i in range(tiles):
-            for j in range(tiles):
-                value = lags[i - j] if i >= j else jnp.zeros((LANES, LANES), BF16)
-                toeplitz[g, i * LANES : (i + 1) * LANES, j * LANES : (j + 1) * LANES] = value
+    half = tok // 2
+
+    def query_steps(some, first):
+        for k in some:
+            q_copy(k).wait()
+        for r in (0, half):
+            total = None
+            for k in some:
+                term = dot(held[k, r : r + half], w_q[k])
+                total = term if total is None else total + term
+            acc_q[r : r + half] = total if first else acc_q[r : r + half] + total
 
     zeros = jnp.zeros((EDGE, chan), BF16)
     prod[:32] = jnp.concatenate([zeros, key_value(proj_kv, EDGE, 32 - EDGE)], axis=0)
     for r in range(32, tok, 32):
         prod[r : r + 32] = key_value(proj_kv, r, 32)
 
-    both = dot(fall[...], prod[...])
-    wide = both[:every] + both[every:]
+    wide = dot(fall[:every], prod[...]) + dot(fall[every:], prod[...])
     group_of = iota((modes, chan), 1) // per_group
     packed = jnp.zeros((modes, chan), F32)
     for g in range(groups):
@@ -254,8 +307,6 @@
     def _():
         mine_state[...] = packed
         swap.start()
-
-    pl.loop(0, groups // 2)(toeplitz_step)
 
     @pl.when(side == 1)
     def _():
@@ -265,10 +316,8 @@
         mine_state[...] = packed + edge_state(rows)
         swap.start()
 
-    pl.loop(groups // 2, groups)(toeplitz_step)
-
-    early = chunks // 2
-    pl.loop(0, early)(query_step)
+    early = max(1, chunks // 4)
+    query_steps(range(early), True)
     decay = jnp.exp(-rate_mc * float(tok))
 
     @pl.when(jnp.logical_and(side == 0, me > 0))
@@ -306,8 +355,7 @@
     def _(i):
         state_copy(pair, pairs - 1 - i).start()
 
-    pl.loop(early, chunks)(query_step)
-
+    query_steps(range(early, chunks), False)
     proj_q[EDGE:] = acc_q[...] * inv
 
     @pl.when(has_next)
@@ -319,27 +367,26 @@
     block = 2 * LANES
 
     def convolve(some):
-        total = []
         for s0 in range(0, tok, block):
             s1 = min(s0 + block, tok)
-            here = None
-            for g in some:
-                part = jnp.where(channel_group[s0:s1] == g, product[s0:s1], jnp.zeros_like(product[s0:s1]))
-                term = dot(toeplitz[g, s0:, s0:s1], part)
-                here = term if here is None else here + term
-            total.append((s0, here))
-        return total
-
-    def add(parts):
-        for s0, value in parts:
-            acc_q[s0:] += value
+            parts = [
+                jnp.where(channel_group[s0:s1] == g, product[s0:s1], jnp.zeros_like(product[s0:s1])) for g in some
+            ]
+            step = (tok - s0) // 2
+            for r in (s0, s0 + step):
+                total = None
+                for g, part in zip(some, parts):
+                    term = dot(toeplitz[g, r : r + step, s0:s1], part)
+                    total = term if total is None else total + term
+                acc_q[r : r + step] += total
 
     acc_q[...] = skip[...] * product.astype(F32)
-    add(convolve(range(groups // 2)))
+    convolve(range(groups // 2))
+    make_rise()
 
     for r in range(32, tok, 32):
         feat_q[r : r + 32] = feature(proj_q, EDGE + r, 32, 0, 0)
-    add(convolve(range(groups // 2, groups)))
+    convolve(range(groups // 2, groups))
 
     pair_decay = jnp.exp(-rate_mc * float(2 * tok))
 
@@ -357,8 +404,11 @@
     stacked = jnp.concatenate([state] * groups, axis=0)
     same = iota((every, chan), 0) // modes == iota((every, chan), 1) // per_group
     high, low = split(jnp.where(same, stacked, 0.0))
-    far = dot(rise[...], jnp.concatenate([high, high], axis=0)) + dot(rise[:, :every], low)
-    out[...] = (feat_q[...] * (acc_q[...] + far)).astype(BF16)
+    paired = jnp.concatenate([high, high], axis=0)
+    for r in (0, half):
+        rows = slice(r, r + half)
+        far = dot(rise[rows], paired) + dot(rise[rows, :every], low)
+        out[rows] = (feat_q[rows] * (acc_q[rows] + far)).astype(BF16)
 
     out_copy.wait()
 
@@ -440,6 +490,7 @@
             pltpu.SemaphoreType.DMA((chunks,)),
             pltpu.SemaphoreType.DMA((chunks,)),
             pltpu.SemaphoreType.DMA((chunks,)),
+            pltpu.SemaphoreType.DMA((chunks,)),
             pltpu.SemaphoreType.DMA((5,)),
             pltpu.SemaphoreType.DMA((5,)),
             pltpu.SemaphoreType.DMA((n // 2,)),

time: 20 us -> 22.4 us (1.12)
  the two profiles are of different devices: /device:TPU:16 before, /device:TPU:17 now
where the time goes in v4:
time: 22.4 us; the launch traced here: 22.3 us
  Pallas kernels  22.3 us (100%)
    pallas_call x1, Pallas kernels, on_device(): pl.pallas_call(functools.partial(mixer, n, depth), out_shape=[pltpu.VMEM(...  19.2 us
    pallas_call x1, Pallas kernels, on_device(): pl.pallas_call(project_out, out_shape=jax.ShapeDtypeStruct((tok, width),...  3.05 us

profile of v4, /device:TPU:17, one launch (start us, length us, event | category | flops | bytes accessed | tf_op | source)
XLA Modules:
  0.0 22.3 jit_solution(16264540124356663913)
XLA Ops:
  0.0 19.2 %mixer.1 = (bf16[384,256]{1,0:T(8,128)(2,1)S(1)}, bf16[256,8192]{1,0:T(8,128)(2,1)S(1)}) custom-call(bf16[384,8192]{1,0:T(8,128)(2,1)} %hidden.1, bf16[8192,768]{1,0:T(8,128)(2,1)} %w_in.1, bf16[256,8192]{1,0:T(8,128)(2,1)} %w_out.1, f32[1,8192]{1,0:T(1,128)} %bitcast.3, f32[7,768]{1,0:T(8,128)} %bitcast.4, f32[8,16]{1,0:T(8,128)} %rates_far.1, ...), custom_call_target="tpu_custom_call" | custom-call | flops 4831838208 | bytes 18874368 | tf_op jit(solution)/shard_map/mixer/pallas_call | solution.py:457
  19.2 3.1 %project_out.1 = bf16[384,8192]{1,0:T(8,128)(2,1)} custom-call(bf16[384,256]{1,0:T(8,128)(2,1)S(1)} %get-tuple-element.7.gated, bf16[256,8192]{1,0:T(8,128)(2,1)S(1)} %get-tuple-element.8.w_out), custom_call_target="tpu_custom_call" | custom-call | flops 1610612736 | bytes 10485760 | tf_op jit(solution)/shard_map/project_out/pallas_call | solution.py:516

commit v5 on v4

--- a/solution.py
+++ b/solution.py
@@ -12,6 +12,7 @@
 LANES = 128
 EDGE = 8
 TAIL = 16
+GROUP = 3
 F32 = jnp.float32
 BF16 = jnp.bfloat16
 
@@ -32,7 +33,7 @@
 def mixer(
     n, depth, hidden, w_in, w_out, gain_far, taps_far, rates_far, residues_far, skip_far, out, w_out_near,
     gain, taps, rates, residues, skip,
-    held, w_kv, w_q, acc_kv, acc_q, squares, proj_kv, proj_q, prod, feat_q,
+    held, w_kv, w_q, tail, acc_kv, acc_q, squares, proj_kv, proj_q, prod, feat_q,
     fall, rise, lag_row, toeplitz, lead, other_lead, edge_fall, mine_state, other_state, even_state, own, slots,
     held_sem, kv_sem, q_sem, tail_sem, near_send, near_recv, send_sem, recv_sem, out_sem, small_sem,
 ):
@@ -57,41 +58,44 @@
     for copy in small:
         copy.start()
 
-    late = chunks // 2
+    late = chunks * 5 // 8
     body = tok - TAIL
 
-    def held_copy(k):
-        cols = pl.ds(pl.multiple_of(k * depth, depth), depth)
-        if k < late:
-            return pltpu.make_async_copy(hidden.at[:, cols], held.at[k], held_sem.at[k])
-        rows = pl.ds(0, body)
+    def held_copy(k, rows):
+        rows, cols = pl.ds(0, rows), pl.ds(pl.multiple_of(k * depth, depth), depth)
         return pltpu.make_async_copy(hidden.at[rows, cols], held.at[k, rows], held_sem.at[k])
 
-    def tail_copy(k):
-        cols = pl.ds(pl.multiple_of(k * depth, depth), depth)
-        rows = pl.ds(body, TAIL)
-        return pltpu.make_async_copy(hidden.at[rows, cols], held.at[k, rows], tail_sem.at[k])
+    tail_copy = pltpu.make_async_copy(
+        hidden.at[pl.ds(body, TAIL), pl.ds(late * depth, width - late * depth)], tail, tail_sem
+    )
 
     def kv_copy(k):
         rows = pl.ds(pl.multiple_of(k * depth, depth), depth)
         return pltpu.make_async_copy(w_in.at[rows, pl.ds(chan, 2 * chan)], w_kv.at[k], kv_sem.at[k])
 
-    def q_copy(k):
-        rows = pl.ds(pl.multiple_of(k * depth, depth), depth)
-        return pltpu.make_async_copy(w_in.at[rows, pl.ds(0, chan)], w_q.at[k], q_sem.at[k])
-
-    for k in range(chunks):
+    parts = 2 if chunks % 2 == 0 else 1
+    deep = width // parts
+
+    def q_copy(i):
+        rows = pl.ds(i * deep, deep)
+        return pltpu.make_async_copy(w_in.at[rows, pl.ds(0, chan)], w_q.at[rows], q_sem.at[i])
+
+    @pl.loop(0, late)
+    def _(k):
+        held_copy(k, tok).start()
         kv_copy(k).start()
-        (held_copy if k < late else tail_copy)(k).start()
-    for k in range(late, chunks):
-        held_copy(k).start()
-
-    @pl.loop(0, chunks)
+
+    tail_copy.start()
+
+    @pl.loop(late, chunks)
     def _(k):
-        q_copy(k).start(priority=1)
+        kv_copy(k).start()
+
+    @pl.loop(late, chunks)
+    def _(k):
+        held_copy(k, body).start()
 
     out_copy = pltpu.make_async_copy(w_out, w_out_near, out_sem)
-    out_copy.start(priority=1)
 
     barrier = pltpu.get_barrier_semaphore()
 
@@ -198,13 +202,18 @@
                 job()
 
     for k in range(late):
-        held_copy(k).wait()
+        held_copy(k, tok).wait()
         kv_copy(k).wait()
         ingest(k, 0, tok)
         beside(k)
+    for i in range(parts):
+        q_copy(i).start(priority=1)
+    out_copy.start(priority=1)
+    tail_copy.wait()
+    for k in range(late, chunks):
+        held[k, body:] = tail[:, (k - late) * depth : (k - late + 1) * depth]
     for k in range(late, chunks):
         kv_copy(k).wait()
-        tail_copy(k).wait()
         ingest(k, body, tok)
 
     def inverse(rows):
@@ -239,7 +248,7 @@
         far_halo.start()
 
     for k in range(late, chunks):
-        held_copy(k).wait()
+        held_copy(k, body).wait()
         ingest(k, 0, body)
         beside(k)
 
@@ -262,12 +271,17 @@
         other_lead[:EDGE] = jnp.zeros((EDGE, 2 * chan), F32)
 
     def feature(buf, r, rows, first, tap_first):
-        total = jnp.zeros((rows, chan), F32)
-        for t in range(taps.shape[0]):
-            total = total + taps[t : t + 1, tap_first : tap_first + chan] * buf[
-                pl.ds(r - t, rows), first : first + chan
-            ]
-        return total
+        shifted = [buf[pl.ds(r - EDGE, EDGE + rows), first : first + chan]]
+        for i in range(1, GROUP):
+            shifted.append(pltpu.roll(shifted[0], i, 0))
+        total = None
+        for t in reversed(range(0, taps.shape[0], GROUP)):
+            if total is not None:
+                total = pltpu.roll(total, GROUP, 0)
+            for i in range(min(GROUP, taps.shape[0] - t)):
+                term = taps[t + i : t + i + 1, tap_first : tap_first + chan] * shifted[i]
+                total = term if total is None else total + term
+        return total[EDGE:]
 
     def key_value(buf, r, rows):
         keyed = feature(buf, r, rows, 0, chan)
@@ -283,19 +297,21 @@
     half = tok // 2
 
     def query_steps(some, first):
-        for k in some:
-            q_copy(k).wait()
+        for i in range(parts):
+            if any(k * depth == i * deep for k in some):
+                q_copy(i).wait()
         for r in (0, half):
             total = None
             for k in some:
-                term = dot(held[k, r : r + half], w_q[k])
+                term = dot(held[k, r : r + half], w_q[k * depth : (k + 1) * depth])
                 total = term if total is None else total + term
             acc_q[r : r + half] = total if first else acc_q[r : r + half] + total
 
     zeros = jnp.zeros((EDGE, chan), BF16)
-    prod[:32] = jnp.concatenate([zeros, key_value(proj_kv, EDGE, 32 - EDGE)], axis=0)
-    for r in range(32, tok, 32):
-        prod[r : r + 32] = key_value(proj_kv, r, 32)
+    strip = 64 if tok % 64 == 0 else 32
+    prod[:strip] = jnp.concatenate([zeros, key_value(proj_kv, EDGE, strip - EDGE)], axis=0)
+    for r in range(strip, tok, strip):
+        prod[r : r + strip] = key_value(proj_kv, r, strip)
 
     wide = dot(fall[:every], prod[...]) + dot(fall[every:], prod[...])
     group_of = iota((modes, chan), 1) // per_group
@@ -316,7 +332,7 @@
         mine_state[...] = packed + edge_state(rows)
         swap.start()
 
-    early = max(1, chunks // 4)
+    early = max(1, chunks * 3 // 8)
     query_steps(range(early), True)
     decay = jnp.exp(-rate_mc * float(tok))
 
@@ -384,8 +400,8 @@
     convolve(range(groups // 2))
     make_rise()
 
-    for r in range(32, tok, 32):
-        feat_q[r : r + 32] = feature(proj_q, EDGE + r, 32, 0, 0)
+    for r in range(strip, tok, strip):
+        feat_q[r : r + strip] = feature(proj_q, EDGE + r, strip, 0, 0)
     convolve(range(groups // 2, groups))
 
     pair_decay = jnp.exp(-rate_mc * float(2 * tok))
@@ -398,7 +414,7 @@
     def _():
         q_halo.wait_recv()
 
-    feat_q[:32] = feature(proj_q, EDGE, 32, 0, 0)
+    feat_q[:strip] = feature(proj_q, EDGE, strip, 0, 0)
     state = lax.fori_loop(0, pair, gather, jnp.zeros((modes, chan), F32))
     state = jnp.where(side == 1, decay * state + even_state[...], state) * weight_mc
     stacked = jnp.concatenate([state] * groups, axis=0)
@@ -467,7 +483,8 @@
             pltpu.VMEM((1, chan), F32),
             pltpu.VMEM((chunks, tok, depth), BF16),
             pltpu.VMEM((chunks, depth, 2 * chan), BF16),
-            pltpu.VMEM((chunks, depth, chan), BF16),
+            pltpu.VMEM((width, chan), BF16),
+            pltpu.VMEM((TAIL, width - chunks * 5 // 8 * depth), BF16),
             pltpu.VMEM((tok, 2 * chan), F32),
             pltpu.VMEM((tok, chan), F32),
             pltpu.VMEM((tok, LANES), F32),
@@ -489,8 +506,8 @@
             pltpu.VMEM((n // 2, modes, chan), BF16),
             pltpu.SemaphoreType.DMA((chunks,)),
             pltpu.SemaphoreType.DMA((chunks,)),
-            pltpu.SemaphoreType.DMA((chunks,)),
-            pltpu.SemaphoreType.DMA((chunks,)),
+            pltpu.SemaphoreType.DMA((2,)),
+            pltpu.SemaphoreType.DMA,
             pltpu.SemaphoreType.DMA((5,)),
             pltpu.SemaphoreType.DMA((5,)),
             pltpu.SemaphoreType.DMA((n // 2,)),

time: 22.4 us -> 18.9 us (0.84)
  Pallas kernels: 22.3 us -> 18.7 us
    pallas_call x1, Pallas kernels: 19.2 us -> 15.6 us  [on_device(): pl.pallas_call(functools.partial(mixer, n, depth), out_shape=[pltpu.VMEM(...]
where the time goes in v5:
time: 18.9 us; the launch traced here: 18.7 us
  Pallas kernels  18.7 us (99%)
    pallas_call x1, Pallas kernels, on_device(): pl.pallas_call(functools.partial(mixer, n, depth), out_shape=[pltpu.VMEM(...  15.6 us
    pallas_call x1, Pallas kernels, on_device(): pl.pallas_call(project_out, out_shape=jax.ShapeDtypeStruct((tok, width),...  3.05 us

profile of v5, /device:TPU:17, one launch (start us, length us, event | category | flops | bytes accessed | tf_op | source)
XLA Modules:
  0.0 18.7 jit_solution(3359840205206501704)
XLA Ops:
  0.0 15.6 %mixer.1 = (bf16[384,256]{1,0:T(8,128)(2,1)S(1)}, bf16[256,8192]{1,0:T(8,128)(2,1)S(1)}) custom-call(bf16[384,8192]{1,0:T(8,128)(2,1)} %hidden.1, bf16[8192,768]{1,0:T(8,128)(2,1)} %w_in.1, bf16[256,8192]{1,0:T(8,128)(2,1)} %w_out.1, f32[1,8192]{1,0:T(1,128)} %bitcast.3, f32[7,768]{1,0:T(8,128)} %bitcast.4, f32[8,16]{1,0:T(8,128)} %rates_far.1, ...), custom_call_target="tpu_custom_call" | custom-call | flops 4831838208 | bytes 18874368 | tf_op jit(solution)/shard_map/mixer/pallas_call | solution.py:473
  15.6 3.1 %project_out.1 = bf16[384,8192]{1,0:T(8,128)(2,1)} custom-call(bf16[384,256]{1,0:T(8,128)(2,1)S(1)} %get-tuple-element.7.gated, bf16[256,8192]{1,0:T(8,128)(2,1)S(1)} %get-tuple-element.8.w_out), custom_call_target="tpu_custom_call" | custom-call | flops 1610612736 | bytes 10485760 | tf_op jit(solution)/shard_map/project_out/pallas_call | solution.py:533

commit v6 on v5

--- a/solution.py
+++ b/solution.py
@@ -35,7 +35,7 @@
     gain, taps, rates, residues, skip,
     held, w_kv, w_q, tail, acc_kv, acc_q, squares, proj_kv, proj_q, prod, feat_q,
     fall, rise, lag_row, toeplitz, lead, other_lead, edge_fall, mine_state, other_state, even_state, own, slots,
-    held_sem, kv_sem, q_sem, tail_sem, near_send, near_recv, send_sem, recv_sem, out_sem, small_sem,
+    load_sem, q_sem, tail_sem, near_recv, recv_sem, out_sem, small_sem,
 ):
     me = lax.axis_index("tm")
     following = lax.rem(me + 1, n)
@@ -63,7 +63,7 @@
 
     def held_copy(k, rows):
         rows, cols = pl.ds(0, rows), pl.ds(pl.multiple_of(k * depth, depth), depth)
-        return pltpu.make_async_copy(hidden.at[rows, cols], held.at[k, rows], held_sem.at[k])
+        return pltpu.make_async_copy(hidden.at[rows, cols], held.at[k, rows], load_sem.at[k])
 
     tail_copy = pltpu.make_async_copy(
         hidden.at[pl.ds(body, TAIL), pl.ds(late * depth, width - late * depth)], tail, tail_sem
@@ -71,7 +71,7 @@
 
     def kv_copy(k):
         rows = pl.ds(pl.multiple_of(k * depth, depth), depth)
-        return pltpu.make_async_copy(w_in.at[rows, pl.ds(chan, 2 * chan)], w_kv.at[k], kv_sem.at[k])
+        return pltpu.make_async_copy(w_in.at[rows, pl.ds(chan, 2 * chan)], w_kv.at[k], load_sem.at[chunks + k])
 
     parts = 2 if chunks % 2 == 0 else 1
     deep = width // parts
@@ -194,7 +194,7 @@
             acc_kv[first:stop] += dot(scaled, w_kv[k])
 
     jobs = [make_lags, make_fall] + [functools.partial(make_toeplitz, [g]) for g in range(groups)]
-    where = [k for k in range(chunks) if 0 < k < chunks - 1] or [0]
+    where = [k for k in range(late) if k > 0] or [0]
 
     def beside(k):
         for i, job in enumerate(jobs):
@@ -225,7 +225,7 @@
 
     def near_copy(i, source, target, device):
         return pltpu.make_async_remote_copy(
-            src_ref=source, dst_ref=target, send_sem=near_send.at[i], recv_sem=near_recv.at[i],
+            src_ref=source, dst_ref=target, send_sem=small_sem.at[i], recv_sem=near_recv.at[i],
             device_id=(device,), device_id_type=MESH,
         )
 
@@ -246,29 +246,6 @@
     @pl.when(sends_far)
     def _():
         far_halo.start()
-
-    for k in range(late, chunks):
-        held_copy(k, body).wait()
-        ingest(k, 0, body)
-        beside(k)
-
-    inv = jnp.concatenate([inverse(slice(0, body)), tail_inv], axis=0)
-    proj_kv[:body] = acc_kv[:body] * inv[:body]
-
-    @pl.when(side == 0)
-    def _():
-        heading.start()
-
-    lead[EDGE:] = proj_kv[:EDGE]
-
-    @pl.when(me == 0)
-    def _():
-        lead[:EDGE] = jnp.zeros((EDGE, 2 * chan), F32)
-        proj_q[:EDGE] = jnp.zeros((EDGE, chan), F32)
-
-    @pl.when(me == 1)
-    def _():
-        other_lead[:EDGE] = jnp.zeros((EDGE, 2 * chan), F32)
 
     def feature(buf, r, rows, first, tap_first):
         shifted = [buf[pl.ds(r - EDGE, EDGE + rows), first : first + chan]]
@@ -294,26 +271,62 @@
             total = total + edge_fall[r] * product[r : r + 1].astype(F32)
         return total
 
+    strip = 64 if tok % 64 == 0 else 32
+    mid = tok // 2 // strip * strip
+    zeros = jnp.zeros((EDGE, chan), BF16)
+    for k in range(late, chunks):
+        held_copy(k, body).wait()
+        ingest(k, 0, mid)
+    for k in range(late, chunks):
+        ingest(k, mid, body)
+    top_inv = inverse(slice(0, mid))
+    proj_kv[:mid] = acc_kv[:mid] * top_inv
+    prod[:strip] = jnp.concatenate([zeros, key_value(proj_kv, EDGE, strip - EDGE)], axis=0)
+    for r in range(strip, mid, strip):
+        prod[r : r + strip] = key_value(proj_kv, r, strip)
+
+    low_inv = inverse(slice(mid, body))
+    proj_kv[mid:body] = acc_kv[mid:body] * low_inv
+    inv = jnp.concatenate([top_inv, low_inv, tail_inv], axis=0)
+
+    @pl.when(side == 0)
+    def _():
+        heading.start()
+
+    lead[EDGE:] = proj_kv[:EDGE]
+
+    @pl.when(me == 0)
+    def _():
+        lead[:EDGE] = jnp.zeros((EDGE, 2 * chan), F32)
+        proj_q[:EDGE] = jnp.zeros((EDGE, chan), F32)
+
+    @pl.when(me == 1)
+    def _():
+        other_lead[:EDGE] = jnp.zeros((EDGE, 2 * chan), F32)
+
     half = tok // 2
 
-    def query_steps(some, first):
+    quarter = tok // 4
+
+    def query_steps(some, starts, first):
         for i in range(parts):
-            if any(k * depth == i * deep for k in some):
+            if starts[0] > 0 and any(k * depth == i * deep for k in some):
                 q_copy(i).wait()
-        for r in (0, half):
+        for r in starts:
             total = None
             for k in some:
-                term = dot(held[k, r : r + half], w_q[k * depth : (k + 1) * depth])
+                term = dot(held[k, r : r + quarter], w_q[k * depth : (k + 1) * depth])
                 total = term if total is None else total + term
-            acc_q[r : r + half] = total if first else acc_q[r : r + half] + total
-
-    zeros = jnp.zeros((EDGE, chan), BF16)
-    strip = 64 if tok % 64 == 0 else 32
-    prod[:strip] = jnp.concatenate([zeros, key_value(proj_kv, EDGE, strip - EDGE)], axis=0)
-    for r in range(strip, tok, strip):
+            acc_q[r : r + quarter] = total if first else acc_q[r : r + quarter] + total
+
+    for r in range(mid, tok, strip):
         prod[r : r + strip] = key_value(proj_kv, r, strip)
 
-    wide = dot(fall[:every], prod[...]) + dot(fall[every:], prod[...])
+    wide = []
+    for m in (0, every // 2):
+        low_part = dot(fall[every + m : every + m + every // 2], prod[...])
+        wide.append(dot(fall[m : m + every // 2], prod[...]) + low_part)
+    wide = jnp.concatenate(wide, axis=0)
     group_of = iota((modes, chan), 1) // per_group
     packed = jnp.zeros((modes, chan), F32)
     for g in range(groups):
@@ -332,8 +345,8 @@
         mine_state[...] = packed + edge_state(rows)
         swap.start()
 
-    early = max(1, chunks * 3 // 8)
-    query_steps(range(early), True)
+    early = max(1, chunks // 2)
+    query_steps(range(early), (half, half + quarter), True)
     decay = jnp.exp(-rate_mc * float(tok))
 
     @pl.when(jnp.logical_and(side == 0, me > 0))
@@ -363,7 +376,7 @@
     def state_copy(source, target):
         return pltpu.make_async_remote_copy(
             src_ref=own, dst_ref=slots.at[source],
-            send_sem=send_sem.at[target], recv_sem=recv_sem.at[source],
+            send_sem=load_sem.at[target], recv_sem=recv_sem.at[source],
             device_id=(2 * target + side,), device_id_type=MESH,
         )
 
@@ -371,12 +384,16 @@
     def _(i):
         state_copy(pair, pairs - 1 - i).start()
 
-    query_steps(range(early, chunks), False)
-    proj_q[EDGE:] = acc_q[...] * inv
+    if early < chunks:
+        query_steps(range(early, chunks), (half, half + quarter), False)
+    proj_q[EDGE + half :] = acc_q[half:] * inv[half:]
 
     @pl.when(has_next)
     def _():
         q_halo.start()
+
+    query_steps(range(chunks), (0, quarter), True)
+    proj_q[EDGE : EDGE + half] = acc_q[:half] * inv[:half]
 
     product = prod[...]
     channel_group = iota((tok, chan), 1) // per_group
@@ -504,13 +521,10 @@
             pltpu.VMEM((modes, chan), F32),
             pltpu.VMEM((modes, chan), BF16),
             pltpu.VMEM((n // 2, modes, chan), BF16),
-            pltpu.SemaphoreType.DMA((chunks,)),
-            pltpu.SemaphoreType.DMA((chunks,)),
+            pltpu.SemaphoreType.DMA((max(2 * chunks, n // 2),)),
             pltpu.SemaphoreType.DMA((2,)),
             pltpu.SemaphoreType.DMA,
             pltpu.SemaphoreType.DMA((5,)),
-            pltpu.SemaphoreType.DMA((5,)),
-            pltpu.SemaphoreType.DMA((n // 2,)),
             pltpu.SemaphoreType.DMA((n // 2,)),
             pltpu.SemaphoreType.DMA,
             pltpu.SemaphoreType.DMA((5,)),

time: 18.9 us -> 18.7 us (0.989)
  Pallas kernels: 18.7 us -> 18.5 us
where the time goes in v6:
time: 18.7 us; the launch traced here: 18.6 us
  Pallas kernels  18.5 us (99%)
    pallas_call x1, Pallas kernels, on_device(): pl.pallas_call(functools.partial(mixer, n, depth), out_shape=[pltpu.VMEM(...  15.5 us
    pallas_call x1, Pallas kernels, on_device(): pl.pallas_call(project_out, out_shape=jax.ShapeDtypeStruct((tok, width),...  3.05 us

profile of v6, /device:TPU:17, one launch (start us, length us, event | category | flops | bytes accessed | tf_op | source)
XLA Modules:
  0.0 18.6 jit_solution(9453762012659264007)
XLA Ops:
  0.0 15.5 %mixer.1 = (bf16[384,256]{1,0:T(8,128)(2,1)S(1)}, bf16[256,8192]{1,0:T(8,128)(2,1)S(1)}) custom-call(bf16[384,8192]{1,0:T(8,128)(2,1)} %hidden.1, bf16[8192,768]{1,0:T(8,128)(2,1)} %w_in.1, bf16[256,8192]{1,0:T(8,128)(2,1)} %w_out.1, f32[1,8192]{1,0:T(1,128)} %bitcast.3, f32[7,768]{1,0:T(8,128)} %bitcast.4, f32[8,16]{1,0:T(8,128)} %rates_far.1, ...), custom_call_target="tpu_custom_call" | custom-call | flops 4831838208 | bytes 18874368 | tf_op jit(solution)/shard_map/mixer/pallas_call | solution.py:490
  15.5 3.1 %project_out.1 = bf16[384,8192]{1,0:T(8,128)(2,1)} custom-call(bf16[384,256]{1,0:T(8,128)(2,1)S(1)} %get-tuple-element.7.gated, bf16[256,8192]{1,0:T(8,128)(2,1)S(1)} %get-tuple-element.8.w_out), custom_call_target="tpu_custom_call" | custom-call | flops 1610612736 | bytes 10485760 | tf_op jit(solution)/shard_map/project_out/pallas_call | solution.py:547

commit v7 on v6

--- a/solution.py
+++ b/solution.py
@@ -34,7 +34,7 @@
     n, depth, hidden, w_in, w_out, gain_far, taps_far, rates_far, residues_far, skip_far, out, w_out_near,
     gain, taps, rates, residues, skip,
     held, w_kv, w_q, tail, acc_kv, acc_q, squares, proj_kv, proj_q, prod, feat_q,
-    fall, rise, lag_row, toeplitz, lead, other_lead, edge_fall, mine_state, other_state, even_state, own, slots,
+    fall, rise, lag_row, toeplitz, lead, other_lead, edge_fall, mine_state, other_state, even_state, own, slots, carried,
     load_sem, q_sem, tail_sem, near_recv, recv_sem, out_sem, small_sem,
 ):
     me = lax.axis_index("tm")
@@ -348,6 +348,15 @@
     early = max(1, chunks // 2)
     query_steps(range(early), (half, half + quarter), True)
     decay = jnp.exp(-rate_mc * float(tok))
+    side_chan = chan // 2
+    low_rows = (half, half + quarter)
+
+    def finish_low():
+        if early < chunks:
+            query_steps(range(early, chunks), low_rows, False)
+        proj_q[EDGE + half :] = acc_q[half:] * inv[half:]
+
+    pl.when(side == 1)(finish_low)
 
     @pl.when(jnp.logical_and(side == 0, me > 0))
     def _():
@@ -359,7 +368,7 @@
         prod[:EDGE] = rows
         whole = packed + edge_state(rows)
         swap.wait_recv()
-        own[...] = (decay * whole + other_state[...]).astype(BF16)
+        own[...] = (decay * whole + other_state[...])[:, :side_chan].astype(BF16)
 
     @pl.when(jnp.logical_and(side == 1, pair > 0))
     def _():
@@ -371,7 +380,7 @@
         swap.wait_recv()
         whole = other_state[...] + edge_state(key_value(other_lead, EDGE, EDGE))
         even_state[...] = whole
-        own[...] = (decay * whole + mine_state[...]).astype(BF16)
+        own[...] = (decay * whole + mine_state[...])[:, side_chan:].astype(BF16)
 
     def state_copy(source, target):
         return pltpu.make_async_remote_copy(
@@ -384,9 +393,7 @@
     def _(i):
         state_copy(pair, pairs - 1 - i).start()
 
-    if early < chunks:
-        query_steps(range(early, chunks), (half, half + quarter), False)
-    proj_q[EDGE + half :] = acc_q[half:] * inv[half:]
+    pl.when(side == 0)(finish_low)
 
     @pl.when(has_next)
     def _():
@@ -422,17 +429,23 @@
     convolve(range(groups // 2, groups))
 
     pair_decay = jnp.exp(-rate_mc * float(2 * tok))
+    pair_decay = jnp.where(side == 1, pair_decay[:, side_chan:], pair_decay[:, :side_chan])
+    trade = near_copy(5, carried.at[side], carried.at[side], sibling)
 
     def gather(p, state):
         state_copy(p, pair).wait_recv()
         return pair_decay * state + slots[p].astype(F32)
 
+    carried[side] = lax.fori_loop(0, pair, gather, jnp.zeros((modes, side_chan), F32))
+    trade.start()
+
     @pl.when(me > 0)
     def _():
         q_halo.wait_recv()
 
     feat_q[:strip] = feature(proj_q, EDGE, strip, 0, 0)
-    state = lax.fori_loop(0, pair, gather, jnp.zeros((modes, chan), F32))
+    trade.wait_recv()
+    state = jnp.concatenate([carried[0], carried[1]], axis=1)
     state = jnp.where(side == 1, decay * state + even_state[...], state) * weight_mc
     stacked = jnp.concatenate([state] * groups, axis=0)
     same = iota((every, chan), 0) // modes == iota((every, chan), 1) // per_group
@@ -446,6 +459,7 @@
     out_copy.wait()
 
     swap.wait_send()
+    trade.wait_send()
 
     @pl.when(has_next)
     def _():
@@ -519,15 +533,16 @@
             pltpu.VMEM((modes, chan), F32),
             pltpu.VMEM((modes, chan), F32),
             pltpu.VMEM((modes, chan), F32),
-            pltpu.VMEM((modes, chan), BF16),
-            pltpu.VMEM((n // 2, modes, chan), BF16),
+            pltpu.VMEM((modes, chan // 2), BF16),
+            pltpu.VMEM((n // 2, modes, chan // 2), BF16),
+            pltpu.VMEM((2, modes, chan // 2), F32),
             pltpu.SemaphoreType.DMA((max(2 * chunks, n // 2),)),
             pltpu.SemaphoreType.DMA((2,)),
             pltpu.SemaphoreType.DMA,
-            pltpu.SemaphoreType.DMA((5,)),
+            pltpu.SemaphoreType.DMA((6,)),
             pltpu.SemaphoreType.DMA((n // 2,)),
             pltpu.SemaphoreType.DMA,
-            pltpu.SemaphoreType.DMA((5,)),
+            pltpu.SemaphoreType.DMA((6,)),
         ],
         compiler_params=pltpu.CompilerParams(
             collective_id=0, has_side_effects=True, vmem_limit_bytes=48 * 1024 * 1024

time: 18.7 us -> 18.8 us (level)
  no operation moved by 1% of the time
where the time goes in v7:
time: 18.8 us; the launch traced here: 18.6 us
  Pallas kernels  18.6 us (99%)
    pallas_call x1, Pallas kernels, on_device(): pl.pallas_call(functools.partial(mixer, n, depth), out_shape=[pltpu.VMEM(...  15.5 us
    pallas_call x1, Pallas kernels, on_device(): pl.pallas_call(project_out, out_shape=jax.ShapeDtypeStruct((tok, width),...  3.05 us

profile of v7, /device:TPU:17, one launch (start us, length us, event | category | flops | bytes accessed | tf_op | source)
XLA Modules:
  0.0 18.6 jit_solution(6130380451469866502)
XLA Ops:
  0.0 15.5 %mixer.1 = (bf16[384,256]{1,0:T(8,128)(2,1)S(1)}, bf16[256,8192]{1,0:T(8,128)(2,1)S(1)}) custom-call(bf16[384,8192]{1,0:T(8,128)(2,1)} %hidden.1, bf16[8192,768]{1,0:T(8,128)(2,1)} %w_in.1, bf16[256,8192]{1,0:T(8,128)(2,1)} %w_out.1, f32[1,8192]{1,0:T(1,128)} %bitcast.3, f32[7,768]{1,0:T(8,128)} %bitcast.4, f32[8,16]{1,0:T(8,128)} %rates_far.1, ...), custom_call_target="tpu_custom_call" | custom-call | flops 4831838208 | bytes 18874368 | tf_op jit(solution)/shard_map/mixer/pallas_call | solution.py:504
  15.5 3.1 %project_out.1 = bf16[384,8192]{1,0:T(8,128)(2,1)} custom-call(bf16[384,256]{1,0:T(8,128)(2,1)S(1)} %get-tuple-element.7.gated, bf16[256,8192]{1,0:T(8,128)(2,1)S(1)} %get-tuple-element.8.w_out), custom_call_target="tpu_custom_call" | custom-call | flops 1610612736 | bytes 10485760 | tf_op jit(solution)/shard_map/project_out/pallas_call | solution.py:562

commit v8 on v7

--- a/solution.py
+++ b/solution.py
@@ -13,6 +13,7 @@
 EDGE = 8
 TAIL = 16
 GROUP = 3
+PARTS = 16
 F32 = jnp.float32
 BF16 = jnp.bfloat16
 
@@ -309,9 +310,6 @@
     quarter = tok // 4
 
     def query_steps(some, starts, first):
-        for i in range(parts):
-            if starts[0] > 0 and any(k * depth == i * deep for k in some):
-                q_copy(i).wait()
         for r in starts:
             total = None
             for k in some:
@@ -345,18 +343,19 @@
         mine_state[...] = packed + edge_state(rows)
         swap.start()
 
-    early = max(1, chunks // 2)
+    early, later = max(1, chunks * 3 // 8), max(1, chunks * 3 // 4)
+    for i in range(parts):
+        q_copy(i).wait()
     query_steps(range(early), (half, half + quarter), True)
     decay = jnp.exp(-rate_mc * float(tok))
     side_chan = chan // 2
     low_rows = (half, half + quarter)
 
-    def finish_low():
-        if early < chunks:
-            query_steps(range(early, chunks), low_rows, False)
-        proj_q[EDGE + half :] = acc_q[half:] * inv[half:]
-
-    pl.when(side == 1)(finish_low)
+    def more_low():
+        if early < later:
+            query_steps(range(early, later), low_rows, False)
+
+    pl.when(side == 1)(more_low)
 
     @pl.when(jnp.logical_and(side == 0, me > 0))
     def _():
@@ -393,7 +392,10 @@
     def _(i):
         state_copy(pair, pairs - 1 - i).start()
 
-    pl.when(side == 0)(finish_low)
+    pl.when(side == 0)(more_low)
+    if later < chunks:
+        query_steps(range(later, chunks), low_rows, False)
+    proj_q[EDGE + half :] = acc_q[half:] * inv[half:]
 
     @pl.when(has_next)
     def _():
@@ -480,16 +482,13 @@
 
 
 def project_out(gated, w_out, mixed, held, sem):
-    parts, _, block = held.shape
-
-    def copy(k):
-        return pltpu.make_async_copy(held.at[k], mixed.at[:, pl.ds(k * block, block)], sem.at[k])
-
-    for k in range(parts):
-        held[k] = dot(gated[...], w_out[:, k * block : (k + 1) * block]).astype(BF16)
-        copy(k).start()
-    for k in range(parts):
-        copy(k).wait()
+    width = mixed.shape[1]
+    block = width // PARTS
+    for k in range(PARTS):
+        cols = slice(k * block, (k + 1) * block)
+        held[:, cols] = dot(gated[...], w_out[:, cols]).astype(BF16)
+        pltpu.make_async_copy(held.at[:, cols], mixed.at[:, cols], sem).start()
+    pltpu.make_async_copy(held, mixed, sem).wait()
 
 
 def on_device(n, hidden, norm_gain, w_in, w_short, residues, rates, skip, w_out):
@@ -558,15 +557,14 @@
             for x in (norm_gain.reshape(1, width), w_short.T, rates, residues, skip.reshape(1, chan))
         ),
     )
-    parts = 16
     return pl.pallas_call(
         project_out,
         out_shape=jax.ShapeDtypeStruct((tok, width), BF16),
         in_specs=[vmem, vmem],
         out_specs=in_hbm,
         scratch_shapes=[
-            pltpu.VMEM((parts, tok, width // parts), BF16),
-            pltpu.SemaphoreType.DMA((parts,)),
+            pltpu.VMEM((tok, width), BF16),
+            pltpu.SemaphoreType.DMA,
         ],
         name="project_out",
         compiler_params=pltpu.CompilerParams(vmem_limit_bytes=24 * 1024 * 1024),

time: 18.8 us -> 18.6 us (0.989)
  the two profiles are of different devices: /device:TPU:17 before, /device:TPU:1 now
where the time goes in v8:
time: 18.6 us; the launch traced here: 18.4 us
  Pallas kernels  18.4 us (99%)
    pallas_call x1, Pallas kernels, on_device(): pl.pallas_call(functools.partial(mixer, n, depth), out_shape=[pltpu.VMEM(...  15.5 us
    pallas_call x1, Pallas kernels, on_device(): pl.pallas_call(project_out, out_shape=jax.ShapeDtypeStruct((tok, width),...  2.92 us

profile of v8, /device:TPU:1, one launch (start us, length us, event | category | flops | bytes accessed | tf_op | source)
XLA Modules:
  0.0 18.4 jit_solution(7776376750975640610)
XLA Ops:
  0.0 15.5 %mixer.1 = (bf16[384,256]{1,0:T(8,128)(2,1)S(1)}, bf16[256,8192]{1,0:T(8,128)(2,1)S(1)}) custom-call(bf16[384,8192]{1,0:T(8,128)(2,1)} %hidden.1, bf16[8192,768]{1,0:T(8,128)(2,1)} %w_in.1, bf16[256,8192]{1,0:T(8,128)(2,1)} %w_out.1, f32[1,8192]{1,0:T(1,128)} %bitcast.3, f32[7,768]{1,0:T(8,128)} %bitcast.4, f32[8,16]{1,0:T(8,128)} %rates_far.1, ...), custom_call_target="tpu_custom_call" | custom-call | flops 4831838208 | bytes 18874368 | tf_op jit(solution)/shard_map/mixer/pallas_call | solution.py:503
  15.5 2.9 %project_out.1 = bf16[384,8192]{1,0:T(8,128)(2,1)} custom-call(bf16[384,256]{1,0:T(8,128)(2,1)S(1)} %get-tuple-element.7.gated, bf16[256,8192]{1,0:T(8,128)(2,1)S(1)} %get-tuple-element.8.w_out), custom_call_target="tpu_custom_call" | custom-call | flops 1610612736 | bytes 10485760 | tf_op jit(solution)/shard_map/project_out/pallas_call | solution.py:560

commit v9 on v8

--- a/solution.py
+++ b/solution.py
@@ -36,7 +36,7 @@
     gain, taps, rates, residues, skip,
     held, w_kv, w_q, tail, acc_kv, acc_q, squares, proj_kv, proj_q, prod, feat_q,
     fall, rise, lag_row, toeplitz, lead, other_lead, edge_fall, mine_state, other_state, even_state, own, slots, carried,
-    load_sem, q_sem, tail_sem, near_recv, recv_sem, out_sem, small_sem,
+    load_sem, near_recv, recv_sem, small_sem,
 ):
     me = lax.axis_index("tm")
     following = lax.rem(me + 1, n)
@@ -59,7 +59,7 @@
     for copy in small:
         copy.start()
 
-    late = chunks * 5 // 8
+    late = chunks * 6 // 8
     body = tok - TAIL
 
     def held_copy(k, rows):
@@ -67,7 +67,7 @@
         return pltpu.make_async_copy(hidden.at[rows, cols], held.at[k, rows], load_sem.at[k])
 
     tail_copy = pltpu.make_async_copy(
-        hidden.at[pl.ds(body, TAIL), pl.ds(late * depth, width - late * depth)], tail, tail_sem
+        hidden.at[pl.ds(body, TAIL), pl.ds(late * depth, width - late * depth)], tail, small_sem.at[5]
     )
 
     def kv_copy(k):
@@ -79,7 +79,7 @@
 
     def q_copy(i):
         rows = pl.ds(i * deep, deep)
-        return pltpu.make_async_copy(w_in.at[rows, pl.ds(0, chan)], w_q.at[rows], q_sem.at[i])
+        return pltpu.make_async_copy(w_in.at[rows, pl.ds(0, chan)], w_q.at[rows], load_sem.at[1 + i])
 
     @pl.loop(0, late)
     def _(k):
@@ -96,7 +96,7 @@
     def _(k):
         held_copy(k, body).start()
 
-    out_copy = pltpu.make_async_copy(w_out, w_out_near, out_sem)
+    out_copy = pltpu.make_async_copy(w_out, w_out_near, load_sem.at[0])
 
     barrier = pltpu.get_barrier_semaphore()
 
@@ -514,7 +514,7 @@
             pltpu.VMEM((chunks, tok, depth), BF16),
             pltpu.VMEM((chunks, depth, 2 * chan), BF16),
             pltpu.VMEM((width, chan), BF16),
-            pltpu.VMEM((TAIL, width - chunks * 5 // 8 * depth), BF16),
+            pltpu.VMEM((TAIL, width - chunks * 6 // 8 * depth), BF16),
             pltpu.VMEM((tok, 2 * chan), F32),
             pltpu.VMEM((tok, chan), F32),
             pltpu.VMEM((tok, LANES), F32),
@@ -536,11 +536,8 @@
             pltpu.VMEM((n // 2, modes, chan // 2), BF16),
             pltpu.VMEM((2, modes, chan // 2), F32),
             pltpu.SemaphoreType.DMA((max(2 * chunks, n // 2),)),
-            pltpu.SemaphoreType.DMA((2,)),
-            pltpu.SemaphoreType.DMA,
             pltpu.SemaphoreType.DMA((6,)),
             pltpu.SemaphoreType.DMA((n // 2,)),
-            pltpu.SemaphoreType.DMA,
             pltpu.SemaphoreType.DMA((6,)),
         ],
         compiler_params=pltpu.CompilerParams(

time: 18.6 us -> 18.2 us (0.978)
  the two profiles are of different devices: /device:TPU:1 before, /device:TPU:17 now
where the time goes in v9:
time: 18.2 us; the launch traced here: 18 us
  Pallas kernels  18 us (99%)
    pallas_call x1, Pallas kernels, on_device(): pl.pallas_call(functools.partial(mixer, n, depth), out_shape=[pltpu.VMEM(...  15.1 us
    pallas_call x1, Pallas kernels, on_device(): pl.pallas_call(project_out, out_shape=jax.ShapeDtypeStruct((tok, width),...  2.92 us

profile of v9, /device:TPU:17, one launch (start us, length us, event | category | flops | bytes accessed | tf_op | source)
XLA Modules:
  0.0 18.0 jit_solution(16635799197599772579)
XLA Ops:
  0.0 15.1 %mixer.1 = (bf16[384,256]{1,0:T(8,128)(2,1)S(1)}, bf16[256,8192]{1,0:T(8,128)(2,1)S(1)}) custom-call(bf16[384,8192]{1,0:T(8,128)(2,1)} %hidden.1, bf16[8192,768]{1,0:T(8,128)(2,1)} %w_in.1, bf16[256,8192]{1,0:T(8,128)(2,1)} %w_out.1, f32[1,8192]{1,0:T(1,128)} %bitcast.3, f32[7,768]{1,0:T(8,128)} %bitcast.4, f32[8,16]{1,0:T(8,128)} %rates_far.1, ...), custom_call_target="tpu_custom_call" | custom-call | flops 4831838208 | bytes 18874368 | tf_op jit(solution)/shard_map/mixer/pallas_call | solution.py:503
  15.1 2.9 %project_out.1 = bf16[384,8192]{1,0:T(8,128)(2,1)} custom-call(bf16[384,256]{1,0:T(8,128)(2,1)S(1)} %get-tuple-element.7.gated, bf16[256,8192]{1,0:T(8,128)(2,1)S(1)} %get-tuple-element.8.w_out), custom_call_target="tpu_custom_call" | custom-call | flops 1610612736 | bytes 10485760 | tf_op jit(solution)/shard_map/project_out/pallas_call | solution.py:557

commit v10 on v9

--- a/solution.py
+++ b/solution.py
@@ -194,7 +194,7 @@
         else:
             acc_kv[first:stop] += dot(scaled, w_kv[k])
 
-    jobs = [make_lags, make_fall] + [functools.partial(make_toeplitz, [g]) for g in range(groups)]
+    jobs = [make_lags, make_fall]
     where = [k for k in range(late) if k > 0] or [0]
 
     def beside(k):
@@ -402,6 +402,7 @@
         q_halo.start()
 
     query_steps(range(chunks), (0, quarter), True)
+    make_toeplitz(range(groups))
     proj_q[EDGE : EDGE + half] = acc_q[:half] * inv[:half]
 
     product = prod[...]

time: 18.2 us -> 18.2 us (level)
  no operation moved by 1% of the time
where the time goes in v10:
time: 18.2 us; the launch traced here: 18 us
  Pallas kernels  18 us (99%)
    pallas_call x1, Pallas kernels, on_device(): pl.pallas_call(functools.partial(mixer, n, depth), out_shape=[pltpu.VMEM(...  15.1 us
    pallas_call x1, Pallas kernels, on_device(): pl.pallas_call(project_out, out_shape=jax.ShapeDtypeStruct((tok, width),...  2.92 us

profile of v10, /device:TPU:17, one launch (start us, length us, event | category | flops | bytes accessed | tf_op | source)
XLA Modules:
  0.0 18.0 jit_solution(6572656283583623145)
XLA Ops:
  0.0 15.1 %mixer.1 = (bf16[384,256]{1,0:T(8,128)(2,1)S(1)}, bf16[256,8192]{1,0:T(8,128)(2,1)S(1)}) custom-call(bf16[384,8192]{1,0:T(8,128)(2,1)} %hidden.1, bf16[8192,768]{1,0:T(8,128)(2,1)} %w_in.1, bf16[256,8192]{1,0:T(8,128)(2,1)} %w_out.1, f32[1,8192]{1,0:T(1,128)} %bitcast.3, f32[7,768]{1,0:T(8,128)} %bitcast.4, f32[8,16]{1,0:T(8,128)} %rates_far.1, ...), custom_call_target="tpu_custom_call" | custom-call | flops 4831838208 | bytes 18874368 | tf_op jit(solution)/shard_map/mixer/pallas_call | solution.py:504
  15.1 2.9 %project_out.1 = bf16[384,8192]{1,0:T(8,128)(2,1)} custom-call(bf16[384,256]{1,0:T(8,128)(2,1)S(1)} %get-tuple-element.7.gated, bf16[256,8192]{1,0:T(8,128)(2,1)S(1)} %get-tuple-element.8.w_out), custom_call_target="tpu_custom_call" | custom-call | flops 1610612736 | bytes 10485760 | tf_op jit(solution)/shard_map/project_out/pallas_call | solution.py:558

commit v11 on v10

--- a/solution.py
+++ b/solution.py
@@ -59,7 +59,7 @@
     for copy in small:
         copy.start()
 
-    late = chunks * 6 // 8
+    late = chunks * 7 // 8
     body = tok - TAIL
 
     def held_copy(k, rows):
@@ -515,7 +515,7 @@
             pltpu.VMEM((chunks, tok, depth), BF16),
             pltpu.VMEM((chunks, depth, 2 * chan), BF16),
             pltpu.VMEM((width, chan), BF16),
-            pltpu.VMEM((TAIL, width - chunks * 6 // 8 * depth), BF16),
+            pltpu.VMEM((TAIL, width - chunks * 7 // 8 * depth), BF16),
             pltpu.VMEM((tok, 2 * chan), F32),
             pltpu.VMEM((tok, chan), F32),
             pltpu.VMEM((tok, LANES), F32),

time: 18.2 us -> 18.1 us (level)
  no operation moved by 1% of the time
where the time goes in v11:
time: 18.1 us; the launch traced here: 17.9 us
  Pallas kernels  17.9 us (99%)
    pallas_call x1, Pallas kernels, on_device(): pl.pallas_call(functools.partial(mixer, n, depth), out_shape=[pltpu.VMEM(...  15 us
    pallas_call x1, Pallas kernels, on_device(): pl.pallas_call(project_out, out_shape=jax.ShapeDtypeStruct((tok, width),...  2.92 us

profile of v11, /device:TPU:17, one launch (start us, length us, event | category | flops | bytes accessed | tf_op | source)
XLA Modules:
  0.0 17.9 jit_solution(17828154909612260942)
XLA Ops:
  0.0 15.0 %mixer.1 = (bf16[384,256]{1,0:T(8,128)(2,1)S(1)}, bf16[256,8192]{1,0:T(8,128)(2,1)S(1)}) custom-call(bf16[384,8192]{1,0:T(8,128)(2,1)} %hidden.1, bf16[8192,768]{1,0:T(8,128)(2,1)} %w_in.1, bf16[256,8192]{1,0:T(8,128)(2,1)} %w_out.1, f32[1,8192]{1,0:T(1,128)} %bitcast.3, f32[7,768]{1,0:T(8,128)} %bitcast.4, f32[8,16]{1,0:T(8,128)} %rates_far.1, ...), custom_call_target="tpu_custom_call" | custom-call | flops 4831838208 | bytes 18874368 | tf_op jit(solution)/shard_map/mixer/pallas_call | solution.py:504
  15.0 2.9 %project_out.1 = bf16[384,8192]{1,0:T(8,128)(2,1)} custom-call(bf16[384,256]{1,0:T(8,128)(2,1)S(1)} %get-tuple-element.7.gated, bf16[256,8192]{1,0:T(8,128)(2,1)S(1)} %get-tuple-element.8.w_out), custom_call_target="tpu_custom_call" | custom-call | flops 1610612736 | bytes 10485760 | tf_op jit(solution)/shard_map/project_out/pallas_call | solution.py:558

commit v12 on v11

--- a/solution.py
+++ b/solution.py
@@ -343,7 +343,7 @@
         mine_state[...] = packed + edge_state(rows)
         swap.start()
 
-    early, later = max(1, chunks * 3 // 8), max(1, chunks * 3 // 4)
+    early, later = max(1, chunks // 4), max(1, chunks * 5 // 8)
     for i in range(parts):
         q_copy(i).wait()
     query_steps(range(early), (half, half + quarter), True)

time: 18.1 us -> 18.1 us (level)
  no operation moved by 1% of the time
where the time goes in v12:
time: 18.1 us; the launch traced here: 17.9 us
  Pallas kernels  17.9 us (99%)
    pallas_call x1, Pallas kernels, on_device(): pl.pallas_call(functools.partial(mixer, n, depth), out_shape=[pltpu.VMEM(...  15 us
    pallas_call x1, Pallas kernels, on_device(): pl.pallas_call(project_out, out_shape=jax.ShapeDtypeStruct((tok, width),...  2.92 us

profile of v12, /device:TPU:17, one launch (start us, length us, event | category | flops | bytes accessed | tf_op | source)
XLA Modules:
  0.0 17.9 jit_solution(16610664713051494395)
XLA Ops:
  0.0 15.0 %mixer.1 = (bf16[384,256]{1,0:T(8,128)(2,1)S(1)}, bf16[256,8192]{1,0:T(8,128)(2,1)S(1)}) custom-call(bf16[384,8192]{1,0:T(8,128)(2,1)} %hidden.1, bf16[8192,768]{1,0:T(8,128)(2,1)} %w_in.1, bf16[256,8192]{1,0:T(8,128)(2,1)} %w_out.1, f32[1,8192]{1,0:T(1,128)} %bitcast.3, f32[7,768]{1,0:T(8,128)} %bitcast.4, f32[8,16]{1,0:T(8,128)} %rates_far.1, ...), custom_call_target="tpu_custom_call" | custom-call | flops 4831838208 | bytes 18874368 | tf_op jit(solution)/shard_map/mixer/pallas_call | solution.py:504
  15.0 2.9 %project_out.1 = bf16[384,8192]{1,0:T(8,128)(2,1)} custom-call(bf16[384,256]{1,0:T(8,128)(2,1)S(1)} %get-tuple-element.7.gated, bf16[256,8192]{1,0:T(8,128)(2,1)S(1)} %get-tuple-element.8.w_out), custom_call_target="tpu_custom_call" | custom-call | flops 1610612736 | bytes 10485760 | tf_op jit(solution)/shard_map/project_out/pallas_call | solution.py:558
